TPU v7x, 256 devices: a whole 4x4x8 slice. The times are simulated.
256 devices in a mesh: pipe: 4 (over y), seq: 16 (over z, core), dp: 4 (over x).
Axes of the slice: x: 4, y: 4, z: 8, core: 2. Of those that a mesh axis runs over, the one named last changes fastest.
Arguments:
- section_inputs: bfloat16 [4, 4, 16, 16, 8, 512], P('pipe', 'dp', 'seq'), may hold values from -6 to 6
- w_spatial: bfloat16 [4, 9, 512, 512], P('pipe'), may hold values from -0.09375 to 0.09375
- w_temporal: bfloat16 [4, 3, 512, 512], P('pipe'), may hold values from -0.15625 to 0.15625
- grad_output: bfloat16 [4, 16, 16, 8, 512], P('dp', 'seq'), may hold values from -6 to 6
- frame_start: int32 [4], P('dp'), may hold values from 0 to 8
- frame_count: int32 [4], P('dp'), may hold values from 9 to 16
Outputs:
- grad_inputs: bfloat16 [4, 4, 16, 16, 8, 512], P('pipe', 'dp', 'seq')
- grad_spatial: float32 [4, 9, 512, 512], P('pipe', None, 'seq')
- grad_temporal: float32 [4, 3, 512, 512], P('pipe', None, 'seq')
Inputs may be any that keep to these rules, and one draw needn't show every extreme that they name: For every clip c, frame_count[c] is greater than frame_start[c].
All inputs are finite; a program needn't handle non-finite values.
Results may differ from a plain program's by a relative error of at most 0.02.
Values may be sent and summed in bfloat16 or wider, within the bound.
No kernel may reach another device: no remote copies, remote signals or barrier semaphores. Data moves between devices by JAX's collectives and lax.ppermute only.
A program may use at most 192 MiB of HBM per device.

v0:
```python
import functools

import jax
import jax.numpy as jnp
from jax import lax
from jax.experimental import pallas as pl
from jax.experimental.pallas import tpu as pltpu
from jax.sharding import PartitionSpec as P


F32 = jnp.float32
BF16 = jnp.bfloat16
ANY = pl.BlockSpec(memory_space=pl.ANY)
SMEM = pl.BlockSpec(memory_space=pltpu.SMEM)
VMEM = pl.BlockSpec(memory_space=pltpu.VMEM)
HBM = pl.BlockSpec(memory_space=pltpu.HBM)

ROWS, COLS, CH = 16, 8, 512
CELLS = ROWS * COLS
FRAMES = 16
CLIPS = 4
SLICE = CH // FRAMES
TAPS = 12
WIDE = TAPS * SLICE
SUB = SLICE // CLIPS


def nn(a, b):
    return lax.dot_general(a, b, (((1,), (0,)), ((), ())), preferred_element_type=F32)


def nt(a, b):
    return lax.dot_general(a, b, (((1,), (1,)), ((), ())), preferred_element_type=F32)


def column_shifts(v):
    col = lax.broadcasted_iota(jnp.int32, v.shape, 0) % COLS
    before = jnp.where(col == 0, 0.0, pltpu.roll(v, 1, 0))
    after = jnp.where(col == COLS - 1, 0.0, pltpu.roll(v, CELLS - 1, 0))
    return {0: v, -1: before, 1: after}


def row_shift(v, step):
    zero = jnp.zeros((COLS, v.shape[1]), v.dtype)
    if step == 0:
        return v
    if step < 0:
        return jnp.concatenate([zero, v[:-COLS]], axis=0)
    return jnp.concatenate([v[COLS:], zero], axis=0)


def forward_kernel(
    x_hbm, wt_hbm, ws_hbm, start_ref, count_ref, mine_ref, slope_ref, wtt_ref, wst_ref, keep_ref,
    x_ref, wt, ws, sems
):
    fetch = pltpu.make_async_copy(x_hbm, x_ref, sems.at[TAPS])
    fetch.start()
    copies = [pltpu.make_async_copy(ws_hbm.at[k], ws.at[k], sems.at[k]) for k in range(9)]
    copies += [pltpu.make_async_copy(wt_hbm.at[k], wt.at[k], sems.at[9 + k]) for k in range(3)]
    for c in copies:
        c.start()
    fetch.wait()
    x = x_ref[...].astype(F32)
    cols = column_shifts(x)
    mine_ref[0] = x.T.astype(BF16)
    pre = None
    for r in range(3):
        for q in range(3):
            k = 3 * r + q
            lhs = row_shift(cols[q - 1], r - 1).astype(BF16)
            copies[k].wait()
            term = nn(lhs, ws[k])
            pre = term if pre is None else pre + term
            wst_ref[k] = ws[k].T
    s = jax.nn.sigmoid(pre)
    slope_ref[...] = s * (1.0 + pre * (1.0 - s))
    mine_ref[1] = (pre * s).astype(BF16).astype(F32).T.astype(BF16)
    for k in range(3):
        copies[9 + k].wait()
        wtt_ref[k] = wt[k].T
    seq = lax.axis_index("seq")
    last = lax.axis_index("pipe") == lax.axis_size("pipe") - 1
    t = seq + lax.broadcasted_iota(jnp.int32, (8, CH), 0)
    low = jnp.where(last, start_ref[0], 0)
    high = jnp.where(last, count_ref[0], FRAMES)
    keep_ref[...] = ((t >= low) & (t < high)).astype(F32)


def forward(x, wt, ws, start, count):
    return pl.pallas_call(
        forward_kernel,
        name="block_forward",
        out_shape=(
            jax.ShapeDtypeStruct((2, CH, CELLS), BF16),
            jax.ShapeDtypeStruct((CELLS, CH), F32),
            jax.ShapeDtypeStruct((3, CH, CH), BF16),
            jax.ShapeDtypeStruct((9, CH, CH), BF16),
            jax.ShapeDtypeStruct((8, CH), F32),
        ),
        in_specs=[HBM] * 3 + [SMEM] * 2,
        out_specs=(VMEM,) * 5,
        scratch_shapes=[
            pltpu.VMEM((CELLS, CH), BF16),
            pltpu.VMEM((3, CH, CH), BF16),
            pltpu.VMEM((9, CH, CH), BF16),
            pltpu.SemaphoreType.DMA((TAPS + 1,)),
        ],
        compiler_params=pltpu.CompilerParams(vmem_limit_bytes=24 << 20),
        cost_estimate=pl.CostEstimate(flops=1208000000, bytes_accessed=13000000, transcendentals=65536),
    )(*(pltpu.with_memory_space_constraint(v, pltpu.HBM) for v in (x, wt, ws)), start, count)


def cotangents(count, refs):
    keep_ref = refs[0]
    own = refs[1:4]
    got = refs[4 : 4 + count]
    last = lax.axis_index("pipe") == lax.axis_size("pipe") - 1
    out = []
    for k in range(3):
        value = own[k][...]
        if count:
            value = jnp.where(last, value, got[k][...])
        keep = keep_ref[k : k + 1, :] != 0.0
        out.append(jnp.where(keep, value.astype(F32), 0.0).astype(BF16))
    return out, refs[4 + count :]


def grad_pre_of(cot, slope_ref, wtt_ref):
    grad_act = nn(cot[0], wtt_ref[0]) + nn(cot[1], wtt_ref[1]) + nn(cot[2], wtt_ref[2])
    return (grad_act.astype(BF16).astype(F32) * slope_ref[...]).astype(BF16)


def spread_of(cot, grad_pre, wst_ref):
    cols = column_shifts(grad_pre.astype(F32))
    total = cot.astype(F32)
    for r in range(3):
        for q in range(3):
            lhs = row_shift(cols[1 - q], 1 - r).astype(BF16)
            total = total + nn(lhs, wst_ref[3 * r + q])
    return total.astype(BF16)


def section_kernel(count, *refs):
    cot, (slope_ref, wtt_ref, wst_ref, gin_ref) = cotangents(count, refs)
    grad_pre = grad_pre_of(cot, slope_ref, wtt_ref)
    gin_ref[...] = spread_of(cot[0], grad_pre, wst_ref)


def emit_kernel(count, *refs):
    cot, (slope_ref, wtt_ref, late_ref, cot_ref, pre_ref) = cotangents(count, refs)
    grad_pre = grad_pre_of(cot, slope_ref, wtt_ref)
    late_ref[:, :SLICE] = grad_pre.astype(F32).T.astype(BF16).reshape(FRAMES, SLICE, CELLS)
    late_ref[:, SLICE:] = cot[0].astype(F32).T.astype(BF16).reshape(FRAMES, SLICE, CELLS)
    cot_ref[...] = cot[0]
    pre_ref[...] = grad_pre


def spread_kernel(cot_ref, pre_ref, wst_ref, gin_ref):
    gin_ref[...] = spread_of(cot_ref[...], pre_ref[...], wst_ref)


def pick_kernel(two_ref, none_ref, out_ref):
    first = lax.axis_index("seq") % 2 == 0
    out_ref[...] = jnp.where(first, two_ref[...], none_ref[...])


def small(kernel, outs, args, specs, flops, read):
    return pl.pallas_call(
        kernel,
        out_shape=tuple(jax.ShapeDtypeStruct(o, BF16) for o in outs),
        in_specs=specs,
        out_specs=(VMEM,) * len(outs),
        compiler_params=pltpu.CompilerParams(vmem_limit_bytes=16 << 20),
        cost_estimate=pl.CostEstimate(flops=flops, bytes_accessed=read, transcendentals=0),
    )(*args)


def pack_kernel(*refs):
    pieces, out, sems = refs[:8], refs[8], refs[9]
    copies = [pltpu.make_async_copy(pieces[k], out.at[k], sems.at[k]) for k in range(8)]
    for c in copies:
        c.start()
    for c in copies:
        c.wait()


def pack(pieces):
    return pl.pallas_call(
        pack_kernel,
        name="pack",
        out_shape=jax.ShapeDtypeStruct((8,) + pieces[0].shape, BF16),
        in_specs=[ANY] * 8,
        out_specs=ANY,
        scratch_shapes=[pltpu.SemaphoreType.DMA((8,))],
        compiler_params=pltpu.CompilerParams(vmem_limit_bytes=4 << 20),
        cost_estimate=pl.CostEstimate(flops=0, bytes_accessed=4000000, transcendentals=0),
    )(*pieces)


def tick_kernel(keep_ref, out_ref):
    out_ref[...] = keep_ref[...]


def tick(keep):
    return pl.pallas_call(
        tick_kernel,
        out_shape=jax.ShapeDtypeStruct(keep.shape, keep.dtype),
        in_specs=[VMEM],
        out_specs=VMEM,
        compiler_params=pltpu.CompilerParams(vmem_limit_bytes=1 << 20),
        cost_estimate=pl.CostEstimate(flops=0, bytes_accessed=32768, transcendentals=0),
    )(keep)


def weights_kernel(late_ref, *refs):
    ring = refs[:8]
    swapped = refs[8]
    outs = refs[9:13]
    left, result = refs[13:]
    seq, d = lax.axis_index("seq"), lax.axis_index("dp")
    z, core = seq // 2, seq % 2
    half = FRAMES // 2
    frame = []
    for k in range(half):
        chip = lax.rem(z + k, half)
        frame += [2 * chip + core, 2 * chip + 1 - core]
    g = jnp.stack([late_ref[t, :SLICE] for t in frame]).astype(F32).reshape(FRAMES * SLICE, CELLS)
    lane = lax.broadcasted_iota(jnp.int32, g.shape, 1)
    row, col = lane // COLS, lane % COLS
    for r in range(3):
        for q in range(3):
            dr, dc = r - 1, q - 1
            v = g if dr == 0 and dc == 0 else pltpu.roll(g, (dr * COLS + dc) % CELLS, 1)
            keep = None
            for at, step, size in ((row, dr, ROWS), (col, dc, COLS)):
                if step:
                    good = (at != 0) if step > 0 else (at != size - 1)
                    keep = good if keep is None else keep & good
            if keep is not None:
                v = jnp.where(keep, v, 0.0)
            v = v.astype(BF16).reshape(FRAMES, SLICE, CELLS)
            base = (3 * r + q) * SLICE
            for f in range(FRAMES):
                left[base : base + SLICE, f * CELLS : (f + 1) * CELLS] = v[f]
    for k in range(3):
        base = (9 + k) * SLICE
        for f in range(FRAMES):
            t = frame[f] + k
            v = late_ref[jnp.minimum(t, FRAMES - 1), SLICE:]
            if k:
                v = jnp.where(t < FRAMES, v, jnp.zeros((SLICE, CELLS), BF16))
            left[base : base + SLICE, f * CELLS : (f + 1) * CELLS] = v
    spatial = temporal = None
    for k in range(half):
        here = slice(2 * k * CELLS, 2 * (k + 1) * CELLS)
        x = jnp.concatenate([ring[k][0], swapped[k, 0]], axis=1)
        act = jnp.concatenate([ring[k][1], swapped[k, 1]], axis=1)
        more = nt(x, left[: 9 * SLICE, here])
        spatial = more if spatial is None else spatial + more
        more = nt(act, left[9 * SLICE :, here])
        temporal = more if temporal is None else temporal + more
    result[:, :, :, : 9 * SLICE] = spatial.reshape(FRAMES, CLIPS, SUB, 9 * SLICE)
    result[:, :, :, 9 * SLICE :] = temporal.reshape(FRAMES, CLIPS, SUB, 3 * SLICE)
    for k in range(CLIPS):
        outs[k][...] = result[:, lax.rem(d + k, CLIPS)].astype(BF16)


def weights(late, ring, swapped):
    return pl.pallas_call(
        weights_kernel,
        name="weight_grads",
        out_shape=(jax.ShapeDtypeStruct((FRAMES, SUB, WIDE), BF16),) * CLIPS,
        in_specs=[VMEM] * 10,
        out_specs=(VMEM,) * CLIPS,
        scratch_shapes=[
            pltpu.VMEM((WIDE, FRAMES * CELLS), BF16),
            pltpu.VMEM((FRAMES, CLIPS, SUB, WIDE), F32),
        ],
        compiler_params=pltpu.CompilerParams(vmem_limit_bytes=24 << 20),
        cost_estimate=pl.CostEstimate(flops=1610000000, bytes_accessed=5000000, transcendentals=0),
    )(late, *ring, swapped)


def assemble_kernel(*refs):
    parts, (spatial_ref, temporal_ref) = refs[:CLIPS], refs[CLIPS:]
    d = lax.axis_index("dp")
    for k in range(CLIPS):
        source = lax.rem(d + CLIPS - k, CLIPS)
        rows = pl.ds(pl.multiple_of(source * SUB, SUB), SUB)
        part = parts[k][...].astype(F32)
        for tap in range(TAPS):
            line = jnp.concatenate(
                [part[s, :, tap * SLICE : (tap + 1) * SLICE] for s in range(FRAMES)], axis=-1
            )
            if tap < 9:
                spatial_ref[tap, rows, :] = line
            else:
                temporal_ref[tap - 9, rows, :] = line


def assemble(parts):
    return pl.pallas_call(
        assemble_kernel,
        name="assemble",
        out_shape=(
            jax.ShapeDtypeStruct((9, SLICE, CH), F32),
            jax.ShapeDtypeStruct((3, SLICE, CH), F32),
        ),
        in_specs=[VMEM] * CLIPS,
        out_specs=(VMEM, VMEM),
        compiler_params=pltpu.CompilerParams(vmem_limit_bytes=24 << 20),
        cost_estimate=pl.CostEstimate(flops=1000000, bytes_accessed=1200000, transcendentals=0),
    )(*parts)


def send(value, axes, sizes, step):
    n, m = sizes
    pairs = [
        (a * m + b, (a + step[0]) % n * m + (b + step[1]) % m) for a in range(n) for b in range(m)
    ]
    return lax.ppermute(value, axes, pairs)


def around(value, axis, size, step):
    return lax.ppermute(value, axis, [(i, (i + step) % size) for i in range(size)])


def local(sizes, *args):
    return backward(sizes, *args)


def backward(sizes, section_inputs, w_spatial, w_temporal, grad_output, frame_start, frame_count):
    axes = ("pipe", "seq")
    steps = sizes[0]
    x = section_inputs.reshape(CELLS, CH)
    ws, wt = w_spatial[0], w_temporal[0]
    cot = grad_output.reshape(CELLS, CH)
    ahead2 = send(cot, axes, sizes, (0, -2))
    ahead1 = send(cot, axes, sizes, (0, -1))
    mine, slope, wtt, wst, keep = forward(x, wt, ws, frame_start, frame_count)
    head = [keep, cot, ahead1, ahead2]
    head_specs = [VMEM] * 4
    ring = {0: mine}
    half = FRAMES // 2

    def grow(k):
        ring[-k] = around(ring[1 - k], "seq", FRAMES, 2)
        if k < half // 2:
            ring[k] = around(ring[k - 1], "seq", FRAMES, -2)

    grow(1)
    got = []
    for step in range(steps - 1):
        (grad_in,) = small(
            functools.partial(section_kernel, len(got)),
            [(CELLS, CH)],
            head + got + [slope, wtt, wst],
            head_specs + [VMEM] * (len(got) + 3),
            805000000,
            7000000,
        )
        two = send(grad_in, axes, sizes, (-1, -2))
        none = send(grad_in, axes, sizes, (-1, 0))
        (mid,) = small(pick_kernel, [(CELLS, CH)], [two, none], [VMEM] * 2, 0, 400000)
        one = lax.ppermute(mid, "seq", [(i, i ^ 1) for i in range(FRAMES)])
        got = [none, one, two]
        grow(step + 2)
        head[0] = tick(keep)
    late, cot0, grad_pre = small(
        functools.partial(emit_kernel, len(got)),
        [(FRAMES, 2 * SLICE, CELLS), (CELLS, CH), (CELLS, CH)],
        head + got + [slope, wtt],
        head_specs + [VMEM] * (len(got) + 2),
        200000000,
        2000000,
    )
    gathered = lax.all_to_all(late, "seq", 0, 0, tiled=True)
    pieces = [ring[k if k < half // 2 else k - half] for k in range(half)]
    packed = pack(pieces)
    swapped = lax.ppermute(packed, "seq", [(i, i ^ 1) for i in range(FRAMES)])
    (grad_in,) = small(
        spread_kernel, [(CELLS, CH)], [cot0, grad_pre, wst], [VMEM] * 3, 604000000, 5000000
    )
    partial = weights(gathered, pieces, swapped)
    shares = [partial[0]] + [around(partial[k], "dp", CLIPS, k) for k in (1, 2, 3)]
    share = sum(s.astype(F32) for s in shares).astype(BF16)
    share = lax.all_to_all(share, "seq", 0, 0, tiled=True)
    parts = [share] + [around(share, "dp", CLIPS, k) for k in (1, 2, 3)]
    spatial, temporal = assemble(parts)
    return grad_in.reshape(section_inputs.shape), spatial[None], temporal[None]


def solution(mesh):
    sizes = (mesh.shape["pipe"], mesh.shape["seq"])
    placed = (
        P("pipe", "dp", "seq", None, None, None),
        P("pipe", None, None, None),
        P("pipe", None, None, None),
        P("dp", "seq", None, None, None),
        P("dp"),
        P("dp"),
    )
    return jax.shard_map(
        functools.partial(local, sizes),
        mesh=mesh,
        in_specs=placed,
        out_specs=(
            P("pipe", "dp", "seq", None, None, None),
            P("pipe", None, "seq", None),
            P("pipe", None, "seq", None),
        ),
        check_vma=False,
    )
```

profile of v0, /device:TPU:1, one launch (start us, length us, event | category | flops | bytes accessed | tf_op | source)
XLA Modules:
  0.0 139.5 jit_solution(12458047030046441326)
XLA Ops:
  1.9 3.9 %block_forward.1 = (bf16[2,512,128]{2,1,0:T(8,128)(2,1)S(1)}, f32[128,512]{1,0:T(8,128)S(1)}, bf16[3,512,512]{2,1,0:T(8,128)(2,1)S(1)}, bf16[9,512,512]{2,1,0:T(8,128)(2,1)S(1)}, f32[8,512]{1,0:T(8,128)S(1)}) custom-call(bf16[128,512]{1,0:T(8,128)(2,1)} %bitcast.15, bf16[3,512,512]{2,1,0:T(8,128)(2,1)} %bitcast.14, bf16[9,512,512]{2,1,0:T(8,128)(2,1)} %bitcast.13, ...), custom_call_target="tpu_custom_call" | custom-call | flops 1208000000 | bytes 13000000 | tf_op jit(solution)/shard_map/block_forward/pallas_call | solution.py:90
  5.8 2.5 %collective-permute-start.14 = (bf16[2,512,128]{2,1,0:T(8,128)(2,1)S(1)}, bf16[2,512,128]{2,1,0:T(8,128)(2,1)S(1)}, u32[]{:S(2)}, u32[]{:S(2)}) collective-permute-start(bf16[2,512,128]{2,1,0:T(8,128)(2,1)S(1)} %get-tuple-element.24.refs_0_), channel_id=1, source_target_pairs={{0,8},{4,12},{8,16},{12,20},{16,24},{20,28},{24,32},{28,36},{32,40... | collective-permute-start | bytes 786440 | tf_op jit(solution)/shard_map/ppermute | solution.py:325
  8.3 4.0 %collective-permute-start.11 = (bf16[2,512,128]{2,1,0:T(8,128)(2,1)S(1)}, bf16[2,512,128]{2,1,0:T(8,128)(2,1)S(1)}, u32[]{:S(2)}, u32[]{:S(2)}) collective-permute-start(bf16[2,512,128]{2,1,0:T(8,128)(2,1)S(1)} %get-tuple-element.24.refs_0_), channel_id=1, source_target_pairs={{0,56},{4,60},{8,0},{12,4},{16,8},{20,12},{24,16},{28,20},{32,24},... | collective-permute-start | bytes 786440 | tf_op jit(solution)/shard_map/ppermute | solution.py:325
  12.4 5.9 %collective-permute-done.14.refs_7_ = bf16[2,512,128]{2,1,0:T(8,128)(2,1)S(1)} collective-permute-done((bf16[2,512,128]{2,1,0:T(8,128)(2,1)S(1)}, bf16[2,512,128]{2,1,0:T(8,128)(2,1)S(1)}, u32[]{:S(2)}, u32[]{:S(2)}) %collective-permute-start.14) | collective-permute-done | bytes 262176 | tf_op jit(solution)/shard_map/ppermute | solution.py:325
  18.3 2.7 %collective-permute-start.12 = (bf16[2,512,128]{2,1,0:T(8,128)(2,1)S(1)}, bf16[2,512,128]{2,1,0:T(8,128)(2,1)S(1)}, u32[]{:S(2)}, u32[]{:S(2)}) collective-permute-start(bf16[2,512,128]{2,1,0:T(8,128)(2,1)S(1)} %collective-permute-done.11.refs_1_), channel_id=1, source_target_pairs={{0,56},{4,60},{8,0},{12,4},{16,8},{20,12},{24,16},{28,20},{32,24},... | collective-permute-start | bytes 786440 | tf_op jit(solution)/shard_map/ppermute | solution.py:325
  21.0 5.1 %collective-permute-done.15.refs_6_ = bf16[2,512,128]{2,1,0:T(8,128)(2,1)S(1)} collective-permute-done((bf16[2,512,128]{2,1,0:T(8,128)(2,1)S(1)}, bf16[2,512,128]{2,1,0:T(8,128)(2,1)S(1)}, u32[]{:S(2)}, u32[]{:S(2)}) %collective-permute-start.15) | collective-permute-done | bytes 262176 | tf_op jit(solution)/shard_map/ppermute | solution.py:325
  26.1 2.7 %collective-permute-start.13 = (bf16[2,512,128]{2,1,0:T(8,128)(2,1)S(1)}, bf16[2,512,128]{2,1,0:T(8,128)(2,1)S(1)}, u32[]{:S(2)}, u32[]{:S(2)}) collective-permute-start(bf16[2,512,128]{2,1,0:T(8,128)(2,1)S(1)} %collective-permute-done.12.refs_2_), channel_id=1, source_target_pairs={{0,56},{4,60},{8,0},{12,4},{16,8},{20,12},{24,16},{28,20},{32,24},... | collective-permute-start | bytes 786440 | tf_op jit(solution)/shard_map/ppermute | solution.py:325
  28.8 4.3 %collective-permute-done.16.refs_5_ = bf16[2,512,128]{2,1,0:T(8,128)(2,1)S(1)} collective-permute-done((bf16[2,512,128]{2,1,0:T(8,128)(2,1)S(1)}, bf16[2,512,128]{2,1,0:T(8,128)(2,1)S(1)}, u32[]{:S(2)}, u32[]{:S(2)}) %collective-permute-start.16) | collective-permute-done | bytes 262176 | tf_op jit(solution)/shard_map/ppermute | solution.py:325
  33.1 6.4 %collective-permute-done.17.refs_4_ = bf16[2,512,128]{2,1,0:T(8,128)(2,1)S(1)} collective-permute-done((bf16[2,512,128]{2,1,0:T(8,128)(2,1)S(1)}, bf16[2,512,128]{2,1,0:T(8,128)(2,1)S(1)}, u32[]{:S(2)}, u32[]{:S(2)}) %collective-permute-start.17) | collective-permute-done | bytes 262176 | tf_op jit(solution)/shard_map/ppermute | solution.py:325
  39.8 4.2 %collective-permute-start.18 = (bf16[8,2,512,128]{3,2,1,0:T(8,128)(2,1)S(1)}, bf16[8,2,512,128]{3,2,1,0:T(8,128)(2,1)S(1)}, u32[]{:S(2)}, u32[]{:S(2)}) collective-permute-start(bf16[8,2,512,128]{3,2,1,0:T(8,128)(2,1)S(1)} %pack.1), channel_id=1, source_target_pairs={{0,4},{4,0},{8,12},{12,8},{16,20},{20,16},{24,28},{28,24},{32,36},... | collective-permute-start | bytes 6291464 | tf_op jit(solution)/shard_map/ppermute | solution.py:380
  44.1 4.8 %collective-permute-done.1.refs_3_ = bf16[128,512]{1,0:T(8,128)(2,1)S(1)} collective-permute-done((bf16[128,512]{1,0:T(8,128)(2,1)S(1)}, bf16[128,512]{1,0:T(8,128)(2,1)S(1)}, u32[]{:S(2)}, u32[]{:S(2)}) %collective-permute-start.1) | collective-permute-done | bytes 131104 | tf_op jit(solution)/shard_map/ppermute | solution.py:321
  48.9 1.7 %collective-permute-done.refs_2_ = bf16[128,512]{1,0:T(8,128)(2,1)S(1)} collective-permute-done((bf16[128,512]{1,0:T(8,128)(2,1)S(1)}, bf16[128,512]{1,0:T(8,128)(2,1)S(1)}, u32[]{:S(2)}, u32[]{:S(2)}) %collective-permute-start) | collective-permute-done | bytes 131104 | tf_op jit(solution)/shard_map/ppermute | solution.py:321
  51.8 3.7 %collective-permute-start.3 = (bf16[128,512]{1,0:T(8,128)(2,1)S(1)}, bf16[128,512]{1,0:T(8,128)(2,1)S(1)}, u32[]{:S(2)}, u32[]{:S(2)}) collective-permute-start(bf16[128,512]{1,0:T(8,128)(2,1)S(1)} %shard_map.86), channel_id=1, source_target_pairs={{0,248},{4,252},{8,192},{12,196},{16,200},{20,204},{24,208},{28,21... | collective-permute-start | bytes 393224 | tf_op jit(solution)/shard_map/ppermute | solution.py:321
  56.0 2.6 %collective-permute-done.3.two_ref.refs_6_ = bf16[128,512]{1,0:T(8,128)(2,1)S(1)} collective-permute-done((bf16[128,512]{1,0:T(8,128)(2,1)S(1)}, bf16[128,512]{1,0:T(8,128)(2,1)S(1)}, u32[]{:S(2)}, u32[]{:S(2)}) %collective-permute-start.3) | collective-permute-done | bytes 131104 | tf_op jit(solution)/shard_map/ppermute | solution.py:321
  58.6 2.7 %collective-permute-done.2.none_ref.refs_4_ = bf16[128,512]{1,0:T(8,128)(2,1)S(1)} collective-permute-done((bf16[128,512]{1,0:T(8,128)(2,1)S(1)}, bf16[128,512]{1,0:T(8,128)(2,1)S(1)}, u32[]{:S(2)}, u32[]{:S(2)}) %collective-permute-start.2) | collective-permute-done | bytes 131104 | tf_op jit(solution)/shard_map/ppermute | solution.py:321
  64.2 3.9 %collective-permute-start.6 = (bf16[128,512]{1,0:T(8,128)(2,1)S(1)}, bf16[128,512]{1,0:T(8,128)(2,1)S(1)}, u32[]{:S(2)}, u32[]{:S(2)}) collective-permute-start(bf16[128,512]{1,0:T(8,128)(2,1)S(1)} %shard_map.88), channel_id=1, source_target_pairs={{0,248},{4,252},{8,192},{12,196},{16,200},{20,204},{24,208},{28,21... | collective-permute-start | bytes 393224 | tf_op jit(solution)/shard_map/ppermute | solution.py:321
  68.1 2.5 %collective-permute-done.6.two_ref.refs_6_ = bf16[128,512]{1,0:T(8,128)(2,1)S(1)} collective-permute-done((bf16[128,512]{1,0:T(8,128)(2,1)S(1)}, bf16[128,512]{1,0:T(8,128)(2,1)S(1)}, u32[]{:S(2)}, u32[]{:S(2)}) %collective-permute-start.6) | collective-permute-done | bytes 131104 | tf_op jit(solution)/shard_map/ppermute | solution.py:321
  70.6 3.0 %collective-permute-done.5.none_ref.refs_4_ = bf16[128,512]{1,0:T(8,128)(2,1)S(1)} collective-permute-done((bf16[128,512]{1,0:T(8,128)(2,1)S(1)}, bf16[128,512]{1,0:T(8,128)(2,1)S(1)}, u32[]{:S(2)}, u32[]{:S(2)}) %collective-permute-start.5) | collective-permute-done | bytes 131104 | tf_op jit(solution)/shard_map/ppermute | solution.py:321
  76.9 3.6 %collective-permute-start.9 = (bf16[128,512]{1,0:T(8,128)(2,1)S(1)}, bf16[128,512]{1,0:T(8,128)(2,1)S(1)}, u32[]{:S(2)}, u32[]{:S(2)}) collective-permute-start(bf16[128,512]{1,0:T(8,128)(2,1)S(1)} %shard_map.90), channel_id=1, source_target_pairs={{0,248},{4,252},{8,192},{12,196},{16,200},{20,204},{24,208},{28,21... | collective-permute-start | bytes 393224 | tf_op jit(solution)/shard_map/ppermute | solution.py:321
  80.5 2.5 %collective-permute-done.9.two_ref.refs_6_ = bf16[128,512]{1,0:T(8,128)(2,1)S(1)} collective-permute-done((bf16[128,512]{1,0:T(8,128)(2,1)S(1)}, bf16[128,512]{1,0:T(8,128)(2,1)S(1)}, u32[]{:S(2)}, u32[]{:S(2)}) %collective-permute-start.9) | collective-permute-done | bytes 131104 | tf_op jit(solution)/shard_map/ppermute | solution.py:321
  83.0 2.7 %collective-permute-done.8.none_ref.refs_4_ = bf16[128,512]{1,0:T(8,128)(2,1)S(1)} collective-permute-done((bf16[128,512]{1,0:T(8,128)(2,1)S(1)}, bf16[128,512]{1,0:T(8,128)(2,1)S(1)}, u32[]{:S(2)}, u32[]{:S(2)}) %collective-permute-start.8) | collective-permute-done | bytes 131104 | tf_op jit(solution)/shard_map/ppermute | solution.py:321
  85.7 1.4 %collective-permute-start.10 = (bf16[128,512]{1,0:T(8,128)(2,1)S(1)}, bf16[128,512]{1,0:T(8,128)(2,1)S(1)}, u32[]{:S(2)}, u32[]{:S(2)}) collective-permute-start(bf16[128,512]{1,0:T(8,128)(2,1)S(1)} %shard_map.91), channel_id=1, source_target_pairs={{0,4},{4,0},{8,12},{12,8},{16,20},{20,16},{24,28},{28,24},{32,36},... | collective-permute-start | bytes 393224 | tf_op jit(solution)/shard_map/ppermute | solution.py:365
  88.6 16.5 %all_to_all.10.late_ref = bf16[16,64,128]{2,1,0:T(8,128)(2,1)S(1)} all-to-all(bf16[16,64,128]{2,1,0:T(8,128)(2,1)S(1)} %get-tuple-element.23), channel_id=1, replica_groups=mesh['pipe'=4,'seq'=16,'dp'=4] {'seq'}, dimensions={0} | all-to-all | bytes 524288 | tf_op jit(solution)/shard_map/all_to_all | solution.py:377
  105.1 2.2 %weight_grads.1 = (bf16[16,8,384]{2,1,0:T(8,128)(2,1)S(1)}, bf16[16,8,384]{2,1,0:T(8,128)(2,1)S(1)}, bf16[16,8,384]{2,1,0:T(8,128)(2,1)S(1)}, bf16[16,8,384]{2,1,0:T(8,128)(2,1)S(1)}) custom-call(bf16[16,64,128]{2,1,0:T(8,128)(2,1)S(1)} %all_to_all.10.late_ref, bf16[2,512,128]{2,1,0:T(8,128)(2,1)S(1)} %get-tuple-element.24.refs_0_, ...), custom_call_target="tpu_custom_call" | custom-call | flops 1610000000 | bytes 5000000 | tf_op jit(solution)/shard_map/weight_grads/pallas_call | solution.py:269
  107.3 1.3 collective-permute-start.19
  108.6 2.5 %collective-permute-start.20 = (bf16[16,8,384]{2,1,0:T(8,128)(2,1)S(1)}, bf16[16,8,384]{2,1,0:T(8,128)(2,1)S(1)}, u32[]{:S(2)}, u32[]{:S(2)}) collective-permute-start(bf16[16,8,384]{2,1,0:T(8,128)(2,1)S(1)} %get-tuple-element.27), channel_id=1, source_target_pairs={{0,2},{1,3},{2,0},{3,1},{4,6},{5,7},{6,4},{7,5},{8,10},{9,11},{10,... | collective-permute-start | bytes 294920 | tf_op jit(solution)/shard_map/ppermute | solution.py:325
  113.3 3.1 %collective-permute-done.20 = bf16[16,8,384]{2,1,0:T(8,128)(2,1)S(1)} collective-permute-done((bf16[16,8,384]{2,1,0:T(8,128)(2,1)S(1)}, bf16[16,8,384]{2,1,0:T(8,128)(2,1)S(1)}, u32[]{:S(2)}, u32[]{:S(2)}) %collective-permute-start.20) | collective-permute-done | bytes 98336 | tf_op jit(solution)/shard_map/ppermute | solution.py:325
  116.5 11.4 %all_to_all.11.refs_0_ = bf16[16,8,384]{2,1,0:T(8,128)(2,1)S(1)} all-to-all(bf16[16,8,384]{2,1,0:T(8,128)(2,1)S(1)} %add_convert_fusion), channel_id=1, replica_groups=mesh['pipe'=4,'seq'=16,'dp'=4] {'seq'}, dimensions={0} | all-to-all | bytes 196608 | tf_op jit(solution)/shard_map/all_to_all | solution.py:387
  127.9 2.0 %collective-permute-start.24 = (bf16[16,8,384]{2,1,0:T(8,128)(2,1)S(1)}, bf16[16,8,384]{2,1,0:T(8,128)(2,1)S(1)}, u32[]{:S(2)}, u32[]{:S(2)}) collective-permute-start(bf16[16,8,384]{2,1,0:T(8,128)(2,1)S(1)} %all_to_all.11.refs_0_), channel_id=1, source_target_pairs={{0,3},{1,0},{2,1},{3,2},{4,7},{5,4},{6,5},{7,6},{8,11},{9,8},{10,9... | collective-permute-start | bytes 294920 | tf_op jit(solution)/shard_map/ppermute | solution.py:325
  131.1 1.4 %shard_map.93 = bf16[128,512]{1,0:T(8,128)(2,1)} custom-call(bf16[128,512]{1,0:T(8,128)(2,1)S(1)} %get-tuple-element.21.cot_ref, bf16[128,512]{1,0:T(8,128)(2,1)S(1)} %get-tuple-element.22.pre_ref, bf16[9,512,512]{2,1,0:T(8,128)(2,1)S(1)} %get-tuple-element.20.refs_6_.refs_9_.wst_ref), custom_call_target="tpu_custom_call" | custom-call | flops 604000000 | bytes 5000000 | tf_op jit(solution)/shard_map/pallas_call | solution.py:168
  132.6 3.0 %collective-permute-done.23.refs_2_ = bf16[16,8,384]{2,1,0:T(8,128)(2,1)S(1)} collective-permute-done((bf16[16,8,384]{2,1,0:T(8,128)(2,1)S(1)}, bf16[16,8,384]{2,1,0:T(8,128)(2,1)S(1)}, u32[]{:S(2)}, u32[]{:S(2)}) %collective-permute-start.23) | collective-permute-done | bytes 98336 | tf_op jit(solution)/shard_map/ppermute | solution.py:325
  135.5 2.7 %collective-permute-done.22.refs_1_ = bf16[16,8,384]{2,1,0:T(8,128)(2,1)S(1)} collective-permute-done((bf16[16,8,384]{2,1,0:T(8,128)(2,1)S(1)}, bf16[16,8,384]{2,1,0:T(8,128)(2,1)S(1)}, u32[]{:S(2)}, u32[]{:S(2)}) %collective-permute-start.22) | collective-permute-done | bytes 98336 | tf_op jit(solution)/shard_map/ppermute | solution.py:325
  (36 shorter events, 14.3 us)
Async XLA Ops:
  5.8 38.2 %copy-start = (bf16[1,1,16,8,512]{4,3,2,1,0:T(8,128)(2,1)S(1)}, bf16[1,1,16,8,512]{4,3,2,1,0:T(8,128)(2,1)}, u32[]{:S(2)}) copy-start(bf16[1,1,16,8,512]{4,3,2,1,0:T(8,128)(2,1)} %param.9) | copy-start | bytes 393220
  5.8 12.5 %collective-permute-start.14 = (bf16[2,512,128]{2,1,0:T(8,128)(2,1)S(1)}, bf16[2,512,128]{2,1,0:T(8,128)(2,1)S(1)}, u32[]{:S(2)}, u32[]{:S(2)}) collective-permute-start(bf16[2,512,128]{2,1,0:T(8,128)(2,1)S(1)} %get-tuple-element.24.refs_0_), channel_id=1, source_target_pairs={{0,8},{4,12},{8,16},{12,20},{16,24},{20,28},{24,32},{28,36},{32,40... | collective-permute-start | bytes 786440 | tf_op jit(solution)/shard_map/ppermute | solution.py:325
  8.3 10.0 %collective-permute-start.11 = (bf16[2,512,128]{2,1,0:T(8,128)(2,1)S(1)}, bf16[2,512,128]{2,1,0:T(8,128)(2,1)S(1)}, u32[]{:S(2)}, u32[]{:S(2)}) collective-permute-start(bf16[2,512,128]{2,1,0:T(8,128)(2,1)S(1)} %get-tuple-element.24.refs_0_), channel_id=1, source_target_pairs={{0,56},{4,60},{8,0},{12,4},{16,8},{20,12},{24,16},{28,20},{32,24},... | collective-permute-start | bytes 786440 | tf_op jit(solution)/shard_map/ppermute | solution.py:325
  18.3 7.8 %collective-permute-start.15 = (bf16[2,512,128]{2,1,0:T(8,128)(2,1)S(1)}, bf16[2,512,128]{2,1,0:T(8,128)(2,1)S(1)}, u32[]{:S(2)}, u32[]{:S(2)}) collective-permute-start(bf16[2,512,128]{2,1,0:T(8,128)(2,1)S(1)} %collective-permute-done.14.refs_7_), channel_id=1, source_target_pairs={{0,8},{4,12},{8,16},{12,20},{16,24},{20,28},{24,32},{28,36},{32,40... | collective-permute-start | bytes 786440 | tf_op jit(solution)/shard_map/ppermute | solution.py:325
  18.3 7.8 %collective-permute-start.12 = (bf16[2,512,128]{2,1,0:T(8,128)(2,1)S(1)}, bf16[2,512,128]{2,1,0:T(8,128)(2,1)S(1)}, u32[]{:S(2)}, u32[]{:S(2)}) collective-permute-start(bf16[2,512,128]{2,1,0:T(8,128)(2,1)S(1)} %collective-permute-done.11.refs_1_), channel_id=1, source_target_pairs={{0,56},{4,60},{8,0},{12,4},{16,8},{20,12},{24,16},{28,20},{32,24},... | collective-permute-start | bytes 786440 | tf_op jit(solution)/shard_map/ppermute | solution.py:325
  26.1 7.0 %collective-permute-start.16 = (bf16[2,512,128]{2,1,0:T(8,128)(2,1)S(1)}, bf16[2,512,128]{2,1,0:T(8,128)(2,1)S(1)}, u32[]{:S(2)}, u32[]{:S(2)}) collective-permute-start(bf16[2,512,128]{2,1,0:T(8,128)(2,1)S(1)} %collective-permute-done.15.refs_6_), channel_id=1, source_target_pairs={{0,8},{4,12},{8,16},{12,20},{16,24},{20,28},{24,32},{28,36},{32,40... | collective-permute-start | bytes 786440 | tf_op jit(solution)/shard_map/ppermute | solution.py:325
  26.1 7.0 %collective-permute-start.13 = (bf16[2,512,128]{2,1,0:T(8,128)(2,1)S(1)}, bf16[2,512,128]{2,1,0:T(8,128)(2,1)S(1)}, u32[]{:S(2)}, u32[]{:S(2)}) collective-permute-start(bf16[2,512,128]{2,1,0:T(8,128)(2,1)S(1)} %collective-permute-done.12.refs_2_), channel_id=1, source_target_pairs={{0,56},{4,60},{8,0},{12,4},{16,8},{20,12},{24,16},{28,20},{32,24},... | collective-permute-start | bytes 786440 | tf_op jit(solution)/shard_map/ppermute | solution.py:325
  33.1 6.4 %collective-permute-start.17 = (bf16[2,512,128]{2,1,0:T(8,128)(2,1)S(1)}, bf16[2,512,128]{2,1,0:T(8,128)(2,1)S(1)}, u32[]{:S(2)}, u32[]{:S(2)}) collective-permute-start(bf16[2,512,128]{2,1,0:T(8,128)(2,1)S(1)} %collective-permute-done.16.refs_5_), channel_id=1, source_target_pairs={{0,8},{4,12},{8,16},{12,20},{16,24},{20,28},{24,32},{28,36},{32,40... | collective-permute-start | bytes 786440 | tf_op jit(solution)/shard_map/ppermute | solution.py:325
  39.8 65.3 %collective-permute-start.18 = (bf16[8,2,512,128]{3,2,1,0:T(8,128)(2,1)S(1)}, bf16[8,2,512,128]{3,2,1,0:T(8,128)(2,1)S(1)}, u32[]{:S(2)}, u32[]{:S(2)}) collective-permute-start(bf16[8,2,512,128]{3,2,1,0:T(8,128)(2,1)S(1)} %pack.1), channel_id=1, source_target_pairs={{0,4},{4,0},{8,12},{12,8},{16,20},{20,16},{24,28},{28,24},{32,36},... | collective-permute-start | bytes 6291464 | tf_op jit(solution)/shard_map/ppermute | solution.py:380
  44.0 5.0 %collective-permute-start.1 = (bf16[128,512]{1,0:T(8,128)(2,1)S(1)}, bf16[128,512]{1,0:T(8,128)(2,1)S(1)}, u32[]{:S(2)}, u32[]{:S(2)}) collective-permute-start(bf16[128,512]{1,0:T(8,128)(2,1)S(1)} %bitcast.7), channel_id=1, source_target_pairs={{0,56},{4,60},{8,0},{12,4},{16,8},{20,12},{24,16},{28,20},{32,24},... | collective-permute-start | bytes 393224 | tf_op jit(solution)/shard_map/ppermute | solution.py:321
  44.0 6.6 %collective-permute-start = (bf16[128,512]{1,0:T(8,128)(2,1)S(1)}, bf16[128,512]{1,0:T(8,128)(2,1)S(1)}, u32[]{:S(2)}, u32[]{:S(2)}) collective-permute-start(bf16[128,512]{1,0:T(8,128)(2,1)S(1)} %bitcast.8), channel_id=1, source_target_pairs={{0,60},{4,0},{8,4},{12,8},{16,12},{20,16},{24,20},{28,24},{32,28},... | collective-permute-start | bytes 393224 | tf_op jit(solution)/shard_map/ppermute | solution.py:321
  51.8 6.8 %collective-permute-start.3 = (bf16[128,512]{1,0:T(8,128)(2,1)S(1)}, bf16[128,512]{1,0:T(8,128)(2,1)S(1)}, u32[]{:S(2)}, u32[]{:S(2)}) collective-permute-start(bf16[128,512]{1,0:T(8,128)(2,1)S(1)} %shard_map.86), channel_id=1, source_target_pairs={{0,248},{4,252},{8,192},{12,196},{16,200},{20,204},{24,208},{28,21... | collective-permute-start | bytes 393224 | tf_op jit(solution)/shard_map/ppermute | solution.py:321
  55.5 5.8 %collective-permute-start.2 = (bf16[128,512]{1,0:T(8,128)(2,1)S(1)}, bf16[128,512]{1,0:T(8,128)(2,1)S(1)}, u32[]{:S(2)}, u32[]{:S(2)}) collective-permute-start(bf16[128,512]{1,0:T(8,128)(2,1)S(1)} %shard_map.86), channel_id=1, source_target_pairs={{0,192},{4,196},{8,200},{12,204},{16,208},{20,212},{24,216},{28,22... | collective-permute-start | bytes 393224 | tf_op jit(solution)/shard_map/ppermute | solution.py:321
  61.4 1.6 %collective-permute-start.4 = (bf16[128,512]{1,0:T(8,128)(2,1)S(1)}, bf16[128,512]{1,0:T(8,128)(2,1)S(1)}, u32[]{:S(2)}, u32[]{:S(2)}) collective-permute-start(bf16[128,512]{1,0:T(8,128)(2,1)S(1)} %shard_map.87), channel_id=1, source_target_pairs={{0,4},{4,0},{8,12},{12,8},{16,20},{20,16},{24,28},{28,24},{32,36},... | collective-permute-start | bytes 393224 | tf_op jit(solution)/shard_map/ppermute | solution.py:365
  64.2 6.4 %collective-permute-start.6 = (bf16[128,512]{1,0:T(8,128)(2,1)S(1)}, bf16[128,512]{1,0:T(8,128)(2,1)S(1)}, u32[]{:S(2)}, u32[]{:S(2)}) collective-permute-start(bf16[128,512]{1,0:T(8,128)(2,1)S(1)} %shard_map.88), channel_id=1, source_target_pairs={{0,248},{4,252},{8,192},{12,196},{16,200},{20,204},{24,208},{28,21... | collective-permute-start | bytes 393224 | tf_op jit(solution)/shard_map/ppermute | solution.py:321
  68.1 5.5 %collective-permute-start.5 = (bf16[128,512]{1,0:T(8,128)(2,1)S(1)}, bf16[128,512]{1,0:T(8,128)(2,1)S(1)}, u32[]{:S(2)}, u32[]{:S(2)}) collective-permute-start(bf16[128,512]{1,0:T(8,128)(2,1)S(1)} %shard_map.88), channel_id=1, source_target_pairs={{0,192},{4,196},{8,200},{12,204},{16,208},{20,212},{24,216},{28,22... | collective-permute-start | bytes 393224 | tf_op jit(solution)/shard_map/ppermute | solution.py:321
  73.6 2.1 %collective-permute-start.7 = (bf16[128,512]{1,0:T(8,128)(2,1)S(1)}, bf16[128,512]{1,0:T(8,128)(2,1)S(1)}, u32[]{:S(2)}, u32[]{:S(2)}) collective-permute-start(bf16[128,512]{1,0:T(8,128)(2,1)S(1)} %shard_map.89), channel_id=1, source_target_pairs={{0,4},{4,0},{8,12},{12,8},{16,20},{20,16},{24,28},{28,24},{32,36},... | collective-permute-start | bytes 393224 | tf_op jit(solution)/shard_map/ppermute | solution.py:365
  76.9 6.1 %collective-permute-start.9 = (bf16[128,512]{1,0:T(8,128)(2,1)S(1)}, bf16[128,512]{1,0:T(8,128)(2,1)S(1)}, u32[]{:S(2)}, u32[]{:S(2)}) collective-permute-start(bf16[128,512]{1,0:T(8,128)(2,1)S(1)} %shard_map.90), channel_id=1, source_target_pairs={{0,248},{4,252},{8,192},{12,196},{16,200},{20,204},{24,208},{28,21... | collective-permute-start | bytes 393224 | tf_op jit(solution)/shard_map/ppermute | solution.py:321
  80.5 5.2 %collective-permute-start.8 = (bf16[128,512]{1,0:T(8,128)(2,1)S(1)}, bf16[128,512]{1,0:T(8,128)(2,1)S(1)}, u32[]{:S(2)}, u32[]{:S(2)}) collective-permute-start(bf16[128,512]{1,0:T(8,128)(2,1)S(1)} %shard_map.90), channel_id=1, source_target_pairs={{0,192},{4,196},{8,200},{12,204},{16,208},{20,212},{24,216},{28,22... | collective-permute-start | bytes 393224 | tf_op jit(solution)/shard_map/ppermute | solution.py:321
  85.7 2.4 %collective-permute-start.10 = (bf16[128,512]{1,0:T(8,128)(2,1)S(1)}, bf16[128,512]{1,0:T(8,128)(2,1)S(1)}, u32[]{:S(2)}, u32[]{:S(2)}) collective-permute-start(bf16[128,512]{1,0:T(8,128)(2,1)S(1)} %shard_map.91), channel_id=1, source_target_pairs={{0,4},{4,0},{8,12},{12,8},{16,20},{20,16},{24,28},{28,24},{32,36},... | collective-permute-start | bytes 393224 | tf_op jit(solution)/shard_map/ppermute | solution.py:365
  107.3 6.0 %collective-permute-start.19 = (bf16[16,8,384]{2,1,0:T(8,128)(2,1)S(1)}, bf16[16,8,384]{2,1,0:T(8,128)(2,1)S(1)}, u32[]{:S(2)}, u32[]{:S(2)}) collective-permute-start(bf16[16,8,384]{2,1,0:T(8,128)(2,1)S(1)} %get-tuple-element.26), channel_id=1, source_target_pairs={{0,1},{1,2},{2,3},{3,0},{4,5},{5,6},{6,7},{7,4},{8,9},{9,10},{10,1... | collective-permute-start | bytes 294920 | tf_op jit(solution)/shard_map/ppermute | solution.py:325
  108.6 7.8 %collective-permute-start.20 = (bf16[16,8,384]{2,1,0:T(8,128)(2,1)S(1)}, bf16[16,8,384]{2,1,0:T(8,128)(2,1)S(1)}, u32[]{:S(2)}, u32[]{:S(2)}) collective-permute-start(bf16[16,8,384]{2,1,0:T(8,128)(2,1)S(1)} %get-tuple-element.27), channel_id=1, source_target_pairs={{0,2},{1,3},{2,0},{3,1},{4,6},{5,7},{6,4},{7,5},{8,10},{9,11},{10,... | collective-permute-start | bytes 294920 | tf_op jit(solution)/shard_map/ppermute | solution.py:325
  111.1 5.3 %collective-permute-start.21 = (bf16[16,8,384]{2,1,0:T(8,128)(2,1)S(1)}, bf16[16,8,384]{2,1,0:T(8,128)(2,1)S(1)}, u32[]{:S(2)}, u32[]{:S(2)}) collective-permute-start(bf16[16,8,384]{2,1,0:T(8,128)(2,1)S(1)} %get-tuple-element.28), channel_id=1, source_target_pairs={{0,3},{1,0},{2,1},{3,2},{4,7},{5,4},{6,5},{7,6},{8,11},{9,8},{10,9... | collective-permute-start | bytes 294920 | tf_op jit(solution)/shard_map/ppermute | solution.py:325
  127.9 4.7 %collective-permute-start.24 = (bf16[16,8,384]{2,1,0:T(8,128)(2,1)S(1)}, bf16[16,8,384]{2,1,0:T(8,128)(2,1)S(1)}, u32[]{:S(2)}, u32[]{:S(2)}) collective-permute-start(bf16[16,8,384]{2,1,0:T(8,128)(2,1)S(1)} %all_to_all.11.refs_0_), channel_id=1, source_target_pairs={{0,3},{1,0},{2,1},{3,2},{4,7},{5,4},{6,5},{7,6},{8,11},{9,8},{10,9... | collective-permute-start | bytes 294920 | tf_op jit(solution)/shard_map/ppermute | solution.py:325
  129.9 5.6 %collective-permute-start.23 = (bf16[16,8,384]{2,1,0:T(8,128)(2,1)S(1)}, bf16[16,8,384]{2,1,0:T(8,128)(2,1)S(1)}, u32[]{:S(2)}, u32[]{:S(2)}) collective-permute-start(bf16[16,8,384]{2,1,0:T(8,128)(2,1)S(1)} %all_to_all.11.refs_0_), channel_id=1, source_target_pairs={{0,2},{1,3},{2,0},{3,1},{4,6},{5,7},{6,4},{7,5},{8,10},{9,11},{10,... | collective-permute-start | bytes 294920 | tf_op jit(solution)/shard_map/ppermute | solution.py:325
  130.7 7.5 %collective-permute-start.22 = (bf16[16,8,384]{2,1,0:T(8,128)(2,1)S(1)}, bf16[16,8,384]{2,1,0:T(8,128)(2,1)S(1)}, u32[]{:S(2)}, u32[]{:S(2)}) collective-permute-start(bf16[16,8,384]{2,1,0:T(8,128)(2,1)S(1)} %all_to_all.11.refs_0_), channel_id=1, source_target_pairs={{0,1},{1,2},{2,3},{3,0},{4,5},{5,6},{6,7},{7,4},{8,9},{9,10},{10,1... | collective-permute-start | bytes 294920 | tf_op jit(solution)/shard_map/ppermute | solution.py:325
where the time goes:
time: 140 us; the launch traced here: 139 us
  waiting for transfers between devices  57.2 us (41%)
  starting transfers between devices  39.2 us (28%)
  blocking collectives  27.9 us (20%)
  Pallas kernels  13 us (9%)
  between operations  2.04 us (1%)
    ppermute x13, waiting for transfers between devices, around(): lax.ppermute(value, axis, [(i, (i + step) % size) for i in range(size)])  31.6 us
    ppermute x8, waiting for transfers between devices, send(): return lax.ppermute(value, axes, pairs)  22.6 us
    ppermute x13, starting transfers between devices, around(): lax.ppermute(value, axis, [(i, (i + step) % size) for i in range(size)])  20.1 us
    all_to_all x1, blocking collectives, backward(): gathered = lax.all_to_all(late, 'seq', 0, 0, tiled=True)  16.5 us
    ppermute x8, starting transfers between devices, send(): return lax.ppermute(value, axes, pairs)  11.8 us
    all_to_all x1, blocking collectives, backward(): share = lax.all_to_all(share, 'seq', 0, 0, tiled=True)  11.4 us
    pallas_call x8, Pallas kernels, small(): pl.pallas_call(kernel, out_shape=tuple((jax.ShapeDtypeStruct(o, BF16) for...  5.52 us
    ppermute x1, starting transfers between devices, backward(): swapped = lax.ppermute(packed, 'seq', [(i, i ^ 1) for i in range(FRAMES)])  4.2 us
  transfers between devices with their start and end apart: 25, of which 19 were waited for; matrix products, arithmetic and copies ran while one was open for 0% of the time, Pallas kernels for 4%

commit v1 on v0

--- a/solution.py
+++ b/solution.py
@@ -49,17 +49,45 @@
     return jnp.concatenate([v[COLS:], zero], axis=0)
 
 
-def forward_kernel(
-    x_hbm, wt_hbm, ws_hbm, start_ref, count_ref, mine_ref, slope_ref, wtt_ref, wst_ref, keep_ref,
-    x_ref, wt, ws, sems
-):
-    fetch = pltpu.make_async_copy(x_hbm, x_ref, sems.at[TAPS])
+def lead_kernel(zero_ref):
+    zero_ref[...] = jnp.zeros((8, CH), F32)
+
+
+def lead():
+    return pl.pallas_call(
+        lead_kernel,
+        name="lead",
+        out_shape=jax.ShapeDtypeStruct((8, CH), F32),
+        out_specs=VMEM,
+        compiler_params=pltpu.CompilerParams(vmem_limit_bytes=1 << 20),
+        cost_estimate=pl.CostEstimate(flops=20000000000, bytes_accessed=16384, transcendentals=0),
+    )()
+
+
+def keep_kernel(start_ref, count_ref, zero_ref, keep_ref):
+    seq = lax.axis_index("seq")
+    last = lax.axis_index("pipe") == lax.axis_size("pipe") - 1
+    t = seq + lax.broadcasted_iota(jnp.int32, (8, CH), 0)
+    low = jnp.where(last, start_ref[0], 0)
+    high = jnp.where(last, count_ref[0], FRAMES)
+    keep_ref[...] = jnp.where((t >= low) & (t < high), 1.0, zero_ref[...])
+
+
+def keep_of(start, count, zeros):
+    return pl.pallas_call(
+        keep_kernel,
+        name="masks",
+        out_shape=jax.ShapeDtypeStruct((8, CH), F32),
+        in_specs=[SMEM] * 2 + [VMEM],
+        out_specs=VMEM,
+        compiler_params=pltpu.CompilerParams(vmem_limit_bytes=1 << 20),
+        cost_estimate=pl.CostEstimate(flops=100, bytes_accessed=16384, transcendentals=0),
+    )(start, count, zeros)
+
+
+def forward_kernel(x_ref, wt, ws, cot_hbm, mine_ref, slope_ref, wtt_ref, wst_ref, cot_ref, sem):
+    fetch = pltpu.make_async_copy(cot_hbm, cot_ref, sem)
     fetch.start()
-    copies = [pltpu.make_async_copy(ws_hbm.at[k], ws.at[k], sems.at[k]) for k in range(9)]
-    copies += [pltpu.make_async_copy(wt_hbm.at[k], wt.at[k], sems.at[9 + k]) for k in range(3)]
-    for c in copies:
-        c.start()
-    fetch.wait()
     x = x_ref[...].astype(F32)
     cols = column_shifts(x)
     mine_ref[0] = x.T.astype(BF16)
@@ -68,7 +96,6 @@
         for q in range(3):
             k = 3 * r + q
             lhs = row_shift(cols[q - 1], r - 1).astype(BF16)
-            copies[k].wait()
             term = nn(lhs, ws[k])
             pre = term if pre is None else pre + term
             wst_ref[k] = ws[k].T
@@ -76,17 +103,11 @@
     slope_ref[...] = s * (1.0 + pre * (1.0 - s))
     mine_ref[1] = (pre * s).astype(BF16).astype(F32).T.astype(BF16)
     for k in range(3):
-        copies[9 + k].wait()
         wtt_ref[k] = wt[k].T
-    seq = lax.axis_index("seq")
-    last = lax.axis_index("pipe") == lax.axis_size("pipe") - 1
-    t = seq + lax.broadcasted_iota(jnp.int32, (8, CH), 0)
-    low = jnp.where(last, start_ref[0], 0)
-    high = jnp.where(last, count_ref[0], FRAMES)
-    keep_ref[...] = ((t >= low) & (t < high)).astype(F32)
-
-
-def forward(x, wt, ws, start, count):
+    fetch.wait()
+
+
+def forward(x, wt, ws, cot):
     return pl.pallas_call(
         forward_kernel,
         name="block_forward",
@@ -95,19 +116,14 @@
             jax.ShapeDtypeStruct((CELLS, CH), F32),
             jax.ShapeDtypeStruct((3, CH, CH), BF16),
             jax.ShapeDtypeStruct((9, CH, CH), BF16),
-            jax.ShapeDtypeStruct((8, CH), F32),
+            jax.ShapeDtypeStruct((CELLS, CH), BF16),
         ),
-        in_specs=[HBM] * 3 + [SMEM] * 2,
+        in_specs=[VMEM] * 3 + [HBM],
         out_specs=(VMEM,) * 5,
-        scratch_shapes=[
-            pltpu.VMEM((CELLS, CH), BF16),
-            pltpu.VMEM((3, CH, CH), BF16),
-            pltpu.VMEM((9, CH, CH), BF16),
-            pltpu.SemaphoreType.DMA((TAPS + 1,)),
-        ],
+        scratch_shapes=[pltpu.SemaphoreType.DMA(())],
         compiler_params=pltpu.CompilerParams(vmem_limit_bytes=24 << 20),
         cost_estimate=pl.CostEstimate(flops=1208000000, bytes_accessed=13000000, transcendentals=65536),
-    )(*(pltpu.with_memory_space_constraint(v, pltpu.HBM) for v in (x, wt, ws)), start, count)
+    )(x, wt, ws, pltpu.with_memory_space_constraint(cot, pltpu.HBM))
 
 
 def cotangents(count, refs):
@@ -335,9 +351,12 @@
     x = section_inputs.reshape(CELLS, CH)
     ws, wt = w_spatial[0], w_temporal[0]
     cot = grad_output.reshape(CELLS, CH)
+    zeros = lead()
     ahead2 = send(cot, axes, sizes, (0, -2))
     ahead1 = send(cot, axes, sizes, (0, -1))
-    mine, slope, wtt, wst, keep = forward(x, wt, ws, frame_start, frame_count)
+    mine, slope, wtt, wst, cot = forward(x, wt, ws, cot)
+    start, count, slope = lax.optimization_barrier((frame_start, frame_count, slope))
+    keep = keep_of(start, count, zeros)
     head = [keep, cot, ahead1, ahead2]
     head_specs = [VMEM] * 4
     ring = {0: mine}

time: 140 us -> 136 us (0.971)
  waiting for transfers between devices: 57.2 us -> 45.7 us
  starting transfers between devices: 39.2 us -> 43.9 us
  local copies, waits for them, and re-layouts: 0.01 us -> 4.64 us
  Pallas kernels: 13 us -> 11 us
    ppermute x13, waiting for transfers between devices: 31.6 us -> 25.4 us  [around(): lax.ppermute(value, axis, [(i, (i + step) % size) for i in range(size)])]
    ppermute x8, waiting for transfers between devices: 22.6 us -> 17.4 us  [send(): return lax.ppermute(value, axes, pairs)]
    ppermute x8, starting transfers between devices: 11.8 us -> 17 us  [send(): return lax.ppermute(value, axes, pairs)]
    unnamed x2 -> x8, local copies, waits for them, and re-layouts: 0.01 us -> 4.64 us
    pallas_call x1, Pallas kernels: 3.87 us -> 1.83 us  [forward(): pl.pallas_call(forward_kernel, name='block_forward', out_shape=(jax.Shape...]
  transfers between devices with their start and end apart: 25 -> 25, of which waited for: 19 -> 17; matrix products, arithmetic and copies ran while one was open for 0% -> 0% of each run, Pallas kernels for 4% -> 4%
where the time goes in v1:
time: 136 us
  waiting for transfers between devices  45.7 us (34%)
  starting transfers between devices  43.9 us (32%)
  blocking collectives  28.2 us (21%)
  Pallas kernels  11 us (8%)
  local copies, waits for them, and re-layouts  4.64 us (3%)
  between operations  2.08 us (2%)
    ppermute x13, waiting for transfers between devices, around(): lax.ppermute(value, axis, [(i, (i + step) % size) for i in range(size)])  25.4 us
    ppermute x13, starting transfers between devices, around(): lax.ppermute(value, axis, [(i, (i + step) % size) for i in range(size)])  20.1 us
    ppermute x8, waiting for transfers between devices, send(): return lax.ppermute(value, axes, pairs)  17.4 us
    ppermute x8, starting transfers between devices, send(): return lax.ppermute(value, axes, pairs)  17 us
    all_to_all x1, blocking collectives, backward(): gathered = lax.all_to_all(late, 'seq', 0, 0, tiled=True)  16.8 us
    all_to_all x1, blocking collectives, backward(): share = lax.all_to_all(share, 'seq', 0, 0, tiled=True)  11.4 us
    pallas_call x8, Pallas kernels, small(): pl.pallas_call(kernel, out_shape=tuple((jax.ShapeDtypeStruct(o, BF16) for...  5.53 us
    unnamed x8, local copies, waits for them, and re-layouts  4.64 us
  transfers between devices with their start and end apart: 25, of which 17 were waited for; matrix products, arithmetic and copies ran while one was open for 0% of the time, Pallas kernels for 4%

profile of v1, /device:TPU:1, one launch (start us, length us, event | category | flops | bytes accessed | tf_op | source)
XLA Modules:
  0.0 135.6 jit_solution(11510647613134402195)
XLA Ops:
  0.6 2.3 %copy-done = bf16[1,9,512,512]{3,2,1,0:T(8,128)(2,1)S(1)} copy-done((bf16[1,9,512,512]{3,2,1,0:T(8,128)(2,1)S(1)}, bf16[1,9,512,512]{3,2,1,0:T(8,128)(2,1)}, u32[]{:S(2)}) %copy-start) | copy-done | bytes 4718616
  3.0 1.4 %copy-done.1 = bf16[1,3,512,512]{3,2,1,0:T(8,128)(2,1)S(1)} copy-done((bf16[1,3,512,512]{3,2,1,0:T(8,128)(2,1)S(1)}, bf16[1,3,512,512]{3,2,1,0:T(8,128)(2,1)}, u32[]{:S(2)}) %copy-start.1) | copy-done | bytes 1572888
  5.3 1.8 %block_forward.1 = (bf16[2,512,128]{2,1,0:T(8,128)(2,1)S(1)}, f32[128,512]{1,0:T(8,128)S(1)}, bf16[3,512,512]{2,1,0:T(8,128)(2,1)S(1)}, bf16[9,512,512]{2,1,0:T(8,128)(2,1)S(1)}, bf16[128,512]{1,0:T(8,128)(2,1)S(1)}) custom-call(bf16[128,512]{1,0:T(8,128)(2,1)S(1)} %bitcast.9, bf16[3,512,512]{2,1,0:T(8,128)(2,1)S(1)} %bitcast.8, ...), custom_call_target="tpu_custom_call" | custom-call | flops 1208000000 | bytes 13000000 | tf_op jit(solution)/shard_map/block_forward/pallas_call | solution.py:111
  7.1 2.5 %collective-permute-start.14 = (bf16[2,512,128]{2,1,0:T(8,128)(2,1)S(1)}, bf16[2,512,128]{2,1,0:T(8,128)(2,1)S(1)}, u32[]{:S(2)}, u32[]{:S(2)}) collective-permute-start(bf16[2,512,128]{2,1,0:T(8,128)(2,1)S(1)} %get-tuple-element.30.refs_0_), channel_id=1, source_target_pairs={{0,8},{4,12},{8,16},{12,20},{16,24},{20,28},{24,32},{28,36},{32,40... | collective-permute-start | bytes 786440 | tf_op jit(solution)/shard_map/ppermute | solution.py:341
  9.7 4.0 %collective-permute-start.11 = (bf16[2,512,128]{2,1,0:T(8,128)(2,1)S(1)}, bf16[2,512,128]{2,1,0:T(8,128)(2,1)S(1)}, u32[]{:S(2)}, u32[]{:S(2)}) collective-permute-start(bf16[2,512,128]{2,1,0:T(8,128)(2,1)S(1)} %get-tuple-element.30.refs_0_), channel_id=1, source_target_pairs={{0,56},{4,60},{8,0},{12,4},{16,8},{20,12},{24,16},{28,20},{32,24},... | collective-permute-start | bytes 786440 | tf_op jit(solution)/shard_map/ppermute | solution.py:341
  13.7 5.9 %collective-permute-done.14.refs_7_ = bf16[2,512,128]{2,1,0:T(8,128)(2,1)S(1)} collective-permute-done((bf16[2,512,128]{2,1,0:T(8,128)(2,1)S(1)}, bf16[2,512,128]{2,1,0:T(8,128)(2,1)S(1)}, u32[]{:S(2)}, u32[]{:S(2)}) %collective-permute-start.14) | collective-permute-done | bytes 262176 | tf_op jit(solution)/shard_map/ppermute | solution.py:341
  19.6 2.7 %collective-permute-start.12 = (bf16[2,512,128]{2,1,0:T(8,128)(2,1)S(1)}, bf16[2,512,128]{2,1,0:T(8,128)(2,1)S(1)}, u32[]{:S(2)}, u32[]{:S(2)}) collective-permute-start(bf16[2,512,128]{2,1,0:T(8,128)(2,1)S(1)} %collective-permute-done.11.refs_1_), channel_id=1, source_target_pairs={{0,56},{4,60},{8,0},{12,4},{16,8},{20,12},{24,16},{28,20},{32,24},... | collective-permute-start | bytes 786440 | tf_op jit(solution)/shard_map/ppermute | solution.py:341
  22.3 5.1 %collective-permute-done.15.refs_6_ = bf16[2,512,128]{2,1,0:T(8,128)(2,1)S(1)} collective-permute-done((bf16[2,512,128]{2,1,0:T(8,128)(2,1)S(1)}, bf16[2,512,128]{2,1,0:T(8,128)(2,1)S(1)}, u32[]{:S(2)}, u32[]{:S(2)}) %collective-permute-start.15) | collective-permute-done | bytes 262176 | tf_op jit(solution)/shard_map/ppermute | solution.py:341
  27.4 2.7 %collective-permute-start.13 = (bf16[2,512,128]{2,1,0:T(8,128)(2,1)S(1)}, bf16[2,512,128]{2,1,0:T(8,128)(2,1)S(1)}, u32[]{:S(2)}, u32[]{:S(2)}) collective-permute-start(bf16[2,512,128]{2,1,0:T(8,128)(2,1)S(1)} %collective-permute-done.12.refs_2_), channel_id=1, source_target_pairs={{0,56},{4,60},{8,0},{12,4},{16,8},{20,12},{24,16},{28,20},{32,24},... | collective-permute-start | bytes 786440 | tf_op jit(solution)/shard_map/ppermute | solution.py:341
  30.1 4.3 %collective-permute-done.16.refs_5_ = bf16[2,512,128]{2,1,0:T(8,128)(2,1)S(1)} collective-permute-done((bf16[2,512,128]{2,1,0:T(8,128)(2,1)S(1)}, bf16[2,512,128]{2,1,0:T(8,128)(2,1)S(1)}, u32[]{:S(2)}, u32[]{:S(2)}) %collective-permute-start.16) | collective-permute-done | bytes 262176 | tf_op jit(solution)/shard_map/ppermute | solution.py:341
  34.4 2.7 %collective-permute-start.1 = (bf16[128,512]{1,0:T(8,128)(2,1)S(1)}, bf16[128,512]{1,0:T(8,128)(2,1)S(1)}, u32[]{:S(2)}, u32[]{:S(2)}) collective-permute-start(bf16[128,512]{1,0:T(8,128)(2,1)S(1)} %bitcast.11), channel_id=1, source_target_pairs={{0,56},{4,60},{8,0},{12,4},{16,8},{20,12},{24,16},{28,20},{32,24},... | collective-permute-start | bytes 393224 | tf_op jit(solution)/shard_map/ppermute | solution.py:337
  37.0 3.5 %collective-permute-start = (bf16[128,512]{1,0:T(8,128)(2,1)S(1)}, bf16[128,512]{1,0:T(8,128)(2,1)S(1)}, u32[]{:S(2)}, u32[]{:S(2)}) collective-permute-start(bf16[128,512]{1,0:T(8,128)(2,1)S(1)} %bitcast.12), channel_id=1, source_target_pairs={{0,60},{4,0},{8,4},{12,8},{16,12},{20,16},{24,20},{28,24},{32,28},... | collective-permute-start | bytes 393224 | tf_op jit(solution)/shard_map/ppermute | solution.py:337
  41.0 4.2 %collective-permute-start.18 = (bf16[8,2,512,128]{3,2,1,0:T(8,128)(2,1)S(1)}, bf16[8,2,512,128]{3,2,1,0:T(8,128)(2,1)S(1)}, u32[]{:S(2)}, u32[]{:S(2)}) collective-permute-start(bf16[8,2,512,128]{3,2,1,0:T(8,128)(2,1)S(1)} %pack.1), channel_id=1, source_target_pairs={{0,4},{4,0},{8,12},{12,8},{16,20},{20,16},{24,28},{28,24},{32,36},... | collective-permute-start | bytes 6291464 | tf_op jit(solution)/shard_map/ppermute | solution.py:399
  47.8 3.2 %collective-permute-start.3 = (bf16[128,512]{1,0:T(8,128)(2,1)S(1)}, bf16[128,512]{1,0:T(8,128)(2,1)S(1)}, u32[]{:S(2)}, u32[]{:S(2)}) collective-permute-start(bf16[128,512]{1,0:T(8,128)(2,1)S(1)} %shard_map.86), channel_id=1, source_target_pairs={{0,248},{4,252},{8,192},{12,196},{16,200},{20,204},{24,208},{28,21... | collective-permute-start | bytes 393224 | tf_op jit(solution)/shard_map/ppermute | solution.py:337
  51.4 2.7 %collective-permute-done.3.two_ref.refs_6_ = bf16[128,512]{1,0:T(8,128)(2,1)S(1)} collective-permute-done((bf16[128,512]{1,0:T(8,128)(2,1)S(1)}, bf16[128,512]{1,0:T(8,128)(2,1)S(1)}, u32[]{:S(2)}, u32[]{:S(2)}) %collective-permute-start.3) | collective-permute-done | bytes 131104 | tf_op jit(solution)/shard_map/ppermute | solution.py:337
  54.0 3.4 %collective-permute-done.2.none_ref.refs_4_ = bf16[128,512]{1,0:T(8,128)(2,1)S(1)} collective-permute-done((bf16[128,512]{1,0:T(8,128)(2,1)S(1)}, bf16[128,512]{1,0:T(8,128)(2,1)S(1)}, u32[]{:S(2)}, u32[]{:S(2)}) %collective-permute-start.2) | collective-permute-done | bytes 131104 | tf_op jit(solution)/shard_map/ppermute | solution.py:337
  60.4 2.6 %collective-permute-start.6 = (bf16[128,512]{1,0:T(8,128)(2,1)S(1)}, bf16[128,512]{1,0:T(8,128)(2,1)S(1)}, u32[]{:S(2)}, u32[]{:S(2)}) collective-permute-start(bf16[128,512]{1,0:T(8,128)(2,1)S(1)} %shard_map.88), channel_id=1, source_target_pairs={{0,248},{4,252},{8,192},{12,196},{16,200},{20,204},{24,208},{28,21... | collective-permute-start | bytes 393224 | tf_op jit(solution)/shard_map/ppermute | solution.py:337
  64.0 2.1 %collective-permute-done.6.two_ref.refs_6_ = bf16[128,512]{1,0:T(8,128)(2,1)S(1)} collective-permute-done((bf16[128,512]{1,0:T(8,128)(2,1)S(1)}, bf16[128,512]{1,0:T(8,128)(2,1)S(1)}, u32[]{:S(2)}, u32[]{:S(2)}) %collective-permute-start.6) | collective-permute-done | bytes 131104 | tf_op jit(solution)/shard_map/ppermute | solution.py:337
  66.1 3.5 %collective-permute-done.5.none_ref.refs_4_ = bf16[128,512]{1,0:T(8,128)(2,1)S(1)} collective-permute-done((bf16[128,512]{1,0:T(8,128)(2,1)S(1)}, bf16[128,512]{1,0:T(8,128)(2,1)S(1)}, u32[]{:S(2)}, u32[]{:S(2)}) %collective-permute-start.5) | collective-permute-done | bytes 131104 | tf_op jit(solution)/shard_map/ppermute | solution.py:337
  72.8 2.6 %collective-permute-start.9 = (bf16[128,512]{1,0:T(8,128)(2,1)S(1)}, bf16[128,512]{1,0:T(8,128)(2,1)S(1)}, u32[]{:S(2)}, u32[]{:S(2)}) collective-permute-start(bf16[128,512]{1,0:T(8,128)(2,1)S(1)} %shard_map.90), channel_id=1, source_target_pairs={{0,248},{4,252},{8,192},{12,196},{16,200},{20,204},{24,208},{28,21... | collective-permute-start | bytes 393224 | tf_op jit(solution)/shard_map/ppermute | solution.py:337
  76.3 2.1 %collective-permute-done.9.two_ref.refs_6_ = bf16[128,512]{1,0:T(8,128)(2,1)S(1)} collective-permute-done((bf16[128,512]{1,0:T(8,128)(2,1)S(1)}, bf16[128,512]{1,0:T(8,128)(2,1)S(1)}, u32[]{:S(2)}, u32[]{:S(2)}) %collective-permute-start.9) | collective-permute-done | bytes 131104 | tf_op jit(solution)/shard_map/ppermute | solution.py:337
  78.4 3.5 %collective-permute-done.8.none_ref.refs_4_ = bf16[128,512]{1,0:T(8,128)(2,1)S(1)} collective-permute-done((bf16[128,512]{1,0:T(8,128)(2,1)S(1)}, bf16[128,512]{1,0:T(8,128)(2,1)S(1)}, u32[]{:S(2)}, u32[]{:S(2)}) %collective-permute-start.8) | collective-permute-done | bytes 131104 | tf_op jit(solution)/shard_map/ppermute | solution.py:337
  84.5 16.8 %all_to_all.10.late_ref = bf16[16,64,128]{2,1,0:T(8,128)(2,1)S(1)} all-to-all(bf16[16,64,128]{2,1,0:T(8,128)(2,1)S(1)} %get-tuple-element.29), channel_id=1, replica_groups=mesh['pipe'=4,'seq'=16,'dp'=4] {'seq'}, dimensions={0} | all-to-all | bytes 524288 | tf_op jit(solution)/shard_map/all_to_all | solution.py:396
  101.3 2.2 %weight_grads.1 = (bf16[16,8,384]{2,1,0:T(8,128)(2,1)S(1)}, bf16[16,8,384]{2,1,0:T(8,128)(2,1)S(1)}, bf16[16,8,384]{2,1,0:T(8,128)(2,1)S(1)}, bf16[16,8,384]{2,1,0:T(8,128)(2,1)S(1)}) custom-call(bf16[16,64,128]{2,1,0:T(8,128)(2,1)S(1)} %all_to_all.10.late_ref, bf16[2,512,128]{2,1,0:T(8,128)(2,1)S(1)} %get-tuple-element.30.refs_0_, ...), custom_call_target="tpu_custom_call" | custom-call | flops 1610000000 | bytes 5000000 | tf_op jit(solution)/shard_map/weight_grads/pallas_call | solution.py:285
  103.5 1.3 collective-permute-start.19
  104.8 2.5 %collective-permute-start.20 = (bf16[16,8,384]{2,1,0:T(8,128)(2,1)S(1)}, bf16[16,8,384]{2,1,0:T(8,128)(2,1)S(1)}, u32[]{:S(2)}, u32[]{:S(2)}) collective-permute-start(bf16[16,8,384]{2,1,0:T(8,128)(2,1)S(1)} %get-tuple-element.33), channel_id=1, source_target_pairs={{0,2},{1,3},{2,0},{3,1},{4,6},{5,7},{6,4},{7,5},{8,10},{9,11},{10,... | collective-permute-start | bytes 294920 | tf_op jit(solution)/shard_map/ppermute | solution.py:341
  109.4 3.1 %collective-permute-done.20 = bf16[16,8,384]{2,1,0:T(8,128)(2,1)S(1)} collective-permute-done((bf16[16,8,384]{2,1,0:T(8,128)(2,1)S(1)}, bf16[16,8,384]{2,1,0:T(8,128)(2,1)S(1)}, u32[]{:S(2)}, u32[]{:S(2)}) %collective-permute-start.20) | collective-permute-done | bytes 98336 | tf_op jit(solution)/shard_map/ppermute | solution.py:341
  112.6 11.4 %all_to_all.11.refs_0_ = bf16[16,8,384]{2,1,0:T(8,128)(2,1)S(1)} all-to-all(bf16[16,8,384]{2,1,0:T(8,128)(2,1)S(1)} %add_convert_fusion), channel_id=1, replica_groups=mesh['pipe'=4,'seq'=16,'dp'=4] {'seq'}, dimensions={0} | all-to-all | bytes 196608 | tf_op jit(solution)/shard_map/all_to_all | solution.py:406
  124.0 2.0 %collective-permute-start.24 = (bf16[16,8,384]{2,1,0:T(8,128)(2,1)S(1)}, bf16[16,8,384]{2,1,0:T(8,128)(2,1)S(1)}, u32[]{:S(2)}, u32[]{:S(2)}) collective-permute-start(bf16[16,8,384]{2,1,0:T(8,128)(2,1)S(1)} %all_to_all.11.refs_0_), channel_id=1, source_target_pairs={{0,3},{1,0},{2,1},{3,2},{4,7},{5,4},{6,5},{7,6},{8,11},{9,8},{10,9... | collective-permute-start | bytes 294920 | tf_op jit(solution)/shard_map/ppermute | solution.py:341
  127.3 1.4 %shard_map.93 = bf16[128,512]{1,0:T(8,128)(2,1)} custom-call(bf16[128,512]{1,0:T(8,128)(2,1)S(1)} %get-tuple-element.27.cot_ref, bf16[128,512]{1,0:T(8,128)(2,1)S(1)} %get-tuple-element.28.pre_ref, bf16[9,512,512]{2,1,0:T(8,128)(2,1)S(1)} %get-tuple-element.26.refs_6_.refs_9_.wst_ref), custom_call_target="tpu_custom_call" | custom-call | flops 604000000 | bytes 5000000 | tf_op jit(solution)/shard_map/pallas_call | solution.py:184
  128.7 3.0 %collective-permute-done.23.refs_2_ = bf16[16,8,384]{2,1,0:T(8,128)(2,1)S(1)} collective-permute-done((bf16[16,8,384]{2,1,0:T(8,128)(2,1)S(1)}, bf16[16,8,384]{2,1,0:T(8,128)(2,1)S(1)}, u32[]{:S(2)}, u32[]{:S(2)}) %collective-permute-start.23) | collective-permute-done | bytes 98336 | tf_op jit(solution)/shard_map/ppermute | solution.py:341
  131.7 2.7 %collective-permute-done.22.refs_1_ = bf16[16,8,384]{2,1,0:T(8,128)(2,1)S(1)} collective-permute-done((bf16[16,8,384]{2,1,0:T(8,128)(2,1)S(1)}, bf16[16,8,384]{2,1,0:T(8,128)(2,1)S(1)}, u32[]{:S(2)}, u32[]{:S(2)}) %collective-permute-start.22) | collective-permute-done | bytes 98336 | tf_op jit(solution)/shard_map/ppermute | solution.py:341
  (44 shorter events, 18.2 us)
Async XLA Ops:
  0.6 2.3 %copy-start = (bf16[1,9,512,512]{3,2,1,0:T(8,128)(2,1)S(1)}, bf16[1,9,512,512]{3,2,1,0:T(8,128)(2,1)}, u32[]{:S(2)}) copy-start(bf16[1,9,512,512]{3,2,1,0:T(8,128)(2,1)} %param.7) | copy-start | bytes 14155780
  3.0 1.4 %copy-start.1 = (bf16[1,3,512,512]{3,2,1,0:T(8,128)(2,1)S(1)}, bf16[1,3,512,512]{3,2,1,0:T(8,128)(2,1)}, u32[]{:S(2)}) copy-start(bf16[1,3,512,512]{3,2,1,0:T(8,128)(2,1)} %param.8) | copy-start | bytes 4718596
  4.4 0.9 copy-start.2
  5.3 29.1 %copy-start.3 = (bf16[1,1,16,8,512]{4,3,2,1,0:T(8,128)(2,1)S(1)}, bf16[1,1,16,8,512]{4,3,2,1,0:T(8,128)(2,1)}, u32[]{:S(2)}) copy-start(bf16[1,1,16,8,512]{4,3,2,1,0:T(8,128)(2,1)} %param.9) | copy-start | bytes 393220
  7.1 12.5 %collective-permute-start.14 = (bf16[2,512,128]{2,1,0:T(8,128)(2,1)S(1)}, bf16[2,512,128]{2,1,0:T(8,128)(2,1)S(1)}, u32[]{:S(2)}, u32[]{:S(2)}) collective-permute-start(bf16[2,512,128]{2,1,0:T(8,128)(2,1)S(1)} %get-tuple-element.30.refs_0_), channel_id=1, source_target_pairs={{0,8},{4,12},{8,16},{12,20},{16,24},{20,28},{24,32},{28,36},{32,40... | collective-permute-start | bytes 786440 | tf_op jit(solution)/shard_map/ppermute | solution.py:341
  9.7 9.9 %collective-permute-start.11 = (bf16[2,512,128]{2,1,0:T(8,128)(2,1)S(1)}, bf16[2,512,128]{2,1,0:T(8,128)(2,1)S(1)}, u32[]{:S(2)}, u32[]{:S(2)}) collective-permute-start(bf16[2,512,128]{2,1,0:T(8,128)(2,1)S(1)} %get-tuple-element.30.refs_0_), channel_id=1, source_target_pairs={{0,56},{4,60},{8,0},{12,4},{16,8},{20,12},{24,16},{28,20},{32,24},... | collective-permute-start | bytes 786440 | tf_op jit(solution)/shard_map/ppermute | solution.py:341
  19.6 7.8 %collective-permute-start.15 = (bf16[2,512,128]{2,1,0:T(8,128)(2,1)S(1)}, bf16[2,512,128]{2,1,0:T(8,128)(2,1)S(1)}, u32[]{:S(2)}, u32[]{:S(2)}) collective-permute-start(bf16[2,512,128]{2,1,0:T(8,128)(2,1)S(1)} %collective-permute-done.14.refs_7_), channel_id=1, source_target_pairs={{0,8},{4,12},{8,16},{12,20},{16,24},{20,28},{24,32},{28,36},{32,40... | collective-permute-start | bytes 786440 | tf_op jit(solution)/shard_map/ppermute | solution.py:341
  19.6 7.8 %collective-permute-start.12 = (bf16[2,512,128]{2,1,0:T(8,128)(2,1)S(1)}, bf16[2,512,128]{2,1,0:T(8,128)(2,1)S(1)}, u32[]{:S(2)}, u32[]{:S(2)}) collective-permute-start(bf16[2,512,128]{2,1,0:T(8,128)(2,1)S(1)} %collective-permute-done.11.refs_1_), channel_id=1, source_target_pairs={{0,56},{4,60},{8,0},{12,4},{16,8},{20,12},{24,16},{28,20},{32,24},... | collective-permute-start | bytes 786440 | tf_op jit(solution)/shard_map/ppermute | solution.py:341
  27.4 7.0 %collective-permute-start.16 = (bf16[2,512,128]{2,1,0:T(8,128)(2,1)S(1)}, bf16[2,512,128]{2,1,0:T(8,128)(2,1)S(1)}, u32[]{:S(2)}, u32[]{:S(2)}) collective-permute-start(bf16[2,512,128]{2,1,0:T(8,128)(2,1)S(1)} %collective-permute-done.15.refs_6_), channel_id=1, source_target_pairs={{0,8},{4,12},{8,16},{12,20},{16,24},{20,28},{24,32},{28,36},{32,40... | collective-permute-start | bytes 786440 | tf_op jit(solution)/shard_map/ppermute | solution.py:341
  27.4 13.2 %collective-permute-start.13 = (bf16[2,512,128]{2,1,0:T(8,128)(2,1)S(1)}, bf16[2,512,128]{2,1,0:T(8,128)(2,1)S(1)}, u32[]{:S(2)}, u32[]{:S(2)}) collective-permute-start(bf16[2,512,128]{2,1,0:T(8,128)(2,1)S(1)} %collective-permute-done.12.refs_2_), channel_id=1, source_target_pairs={{0,56},{4,60},{8,0},{12,4},{16,8},{20,12},{24,16},{28,20},{32,24},... | collective-permute-start | bytes 786440 | tf_op jit(solution)/shard_map/ppermute | solution.py:341
  34.4 6.4 %collective-permute-start.17 = (bf16[2,512,128]{2,1,0:T(8,128)(2,1)S(1)}, bf16[2,512,128]{2,1,0:T(8,128)(2,1)S(1)}, u32[]{:S(2)}, u32[]{:S(2)}) collective-permute-start(bf16[2,512,128]{2,1,0:T(8,128)(2,1)S(1)} %collective-permute-done.16.refs_5_), channel_id=1, source_target_pairs={{0,8},{4,12},{8,16},{12,20},{16,24},{20,28},{24,32},{28,36},{32,40... | collective-permute-start | bytes 786440 | tf_op jit(solution)/shard_map/ppermute | solution.py:341
  34.4 12.2 %collective-permute-start.1 = (bf16[128,512]{1,0:T(8,128)(2,1)S(1)}, bf16[128,512]{1,0:T(8,128)(2,1)S(1)}, u32[]{:S(2)}, u32[]{:S(2)}) collective-permute-start(bf16[128,512]{1,0:T(8,128)(2,1)S(1)} %bitcast.11), channel_id=1, source_target_pairs={{0,56},{4,60},{8,0},{12,4},{16,8},{20,12},{24,16},{28,20},{32,24},... | collective-permute-start | bytes 393224 | tf_op jit(solution)/shard_map/ppermute | solution.py:337
  37.0 9.5 %collective-permute-start = (bf16[128,512]{1,0:T(8,128)(2,1)S(1)}, bf16[128,512]{1,0:T(8,128)(2,1)S(1)}, u32[]{:S(2)}, u32[]{:S(2)}) collective-permute-start(bf16[128,512]{1,0:T(8,128)(2,1)S(1)} %bitcast.12), channel_id=1, source_target_pairs={{0,60},{4,0},{8,4},{12,8},{16,12},{20,16},{24,20},{28,24},{32,28},... | collective-permute-start | bytes 393224 | tf_op jit(solution)/shard_map/ppermute | solution.py:337
  41.0 60.2 %collective-permute-start.18 = (bf16[8,2,512,128]{3,2,1,0:T(8,128)(2,1)S(1)}, bf16[8,2,512,128]{3,2,1,0:T(8,128)(2,1)S(1)}, u32[]{:S(2)}, u32[]{:S(2)}) collective-permute-start(bf16[8,2,512,128]{3,2,1,0:T(8,128)(2,1)S(1)} %pack.1), channel_id=1, source_target_pairs={{0,4},{4,0},{8,12},{12,8},{16,20},{20,16},{24,28},{28,24},{32,36},... | collective-permute-start | bytes 6291464 | tf_op jit(solution)/shard_map/ppermute | solution.py:399
  47.8 6.3 %collective-permute-start.3 = (bf16[128,512]{1,0:T(8,128)(2,1)S(1)}, bf16[128,512]{1,0:T(8,128)(2,1)S(1)}, u32[]{:S(2)}, u32[]{:S(2)}) collective-permute-start(bf16[128,512]{1,0:T(8,128)(2,1)S(1)} %shard_map.86), channel_id=1, source_target_pairs={{0,248},{4,252},{8,192},{12,196},{16,200},{20,204},{24,208},{28,21... | collective-permute-start | bytes 393224 | tf_op jit(solution)/shard_map/ppermute | solution.py:337
  50.9 6.5 %collective-permute-start.2 = (bf16[128,512]{1,0:T(8,128)(2,1)S(1)}, bf16[128,512]{1,0:T(8,128)(2,1)S(1)}, u32[]{:S(2)}, u32[]{:S(2)}) collective-permute-start(bf16[128,512]{1,0:T(8,128)(2,1)S(1)} %shard_map.86), channel_id=1, source_target_pairs={{0,192},{4,196},{8,200},{12,204},{16,208},{20,212},{24,216},{28,22... | collective-permute-start | bytes 393224 | tf_op jit(solution)/shard_map/ppermute | solution.py:337
  57.5 1.7 %collective-permute-start.4 = (bf16[128,512]{1,0:T(8,128)(2,1)S(1)}, bf16[128,512]{1,0:T(8,128)(2,1)S(1)}, u32[]{:S(2)}, u32[]{:S(2)}) collective-permute-start(bf16[128,512]{1,0:T(8,128)(2,1)S(1)} %shard_map.87), channel_id=1, source_target_pairs={{0,4},{4,0},{8,12},{12,8},{16,20},{20,16},{24,28},{28,24},{32,36},... | collective-permute-start | bytes 393224 | tf_op jit(solution)/shard_map/ppermute | solution.py:384
  60.4 5.7 %collective-permute-start.6 = (bf16[128,512]{1,0:T(8,128)(2,1)S(1)}, bf16[128,512]{1,0:T(8,128)(2,1)S(1)}, u32[]{:S(2)}, u32[]{:S(2)}) collective-permute-start(bf16[128,512]{1,0:T(8,128)(2,1)S(1)} %shard_map.88), channel_id=1, source_target_pairs={{0,248},{4,252},{8,192},{12,196},{16,200},{20,204},{24,208},{28,21... | collective-permute-start | bytes 393224 | tf_op jit(solution)/shard_map/ppermute | solution.py:337
  63.0 6.6 %collective-permute-start.5 = (bf16[128,512]{1,0:T(8,128)(2,1)S(1)}, bf16[128,512]{1,0:T(8,128)(2,1)S(1)}, u32[]{:S(2)}, u32[]{:S(2)}) collective-permute-start(bf16[128,512]{1,0:T(8,128)(2,1)S(1)} %shard_map.88), channel_id=1, source_target_pairs={{0,192},{4,196},{8,200},{12,204},{16,208},{20,212},{24,216},{28,22... | collective-permute-start | bytes 393224 | tf_op jit(solution)/shard_map/ppermute | solution.py:337
  69.6 1.9 %collective-permute-start.7 = (bf16[128,512]{1,0:T(8,128)(2,1)S(1)}, bf16[128,512]{1,0:T(8,128)(2,1)S(1)}, u32[]{:S(2)}, u32[]{:S(2)}) collective-permute-start(bf16[128,512]{1,0:T(8,128)(2,1)S(1)} %shard_map.89), channel_id=1, source_target_pairs={{0,4},{4,0},{8,12},{12,8},{16,20},{20,16},{24,28},{28,24},{32,36},... | collective-permute-start | bytes 393224 | tf_op jit(solution)/shard_map/ppermute | solution.py:384
  72.8 5.7 %collective-permute-start.9 = (bf16[128,512]{1,0:T(8,128)(2,1)S(1)}, bf16[128,512]{1,0:T(8,128)(2,1)S(1)}, u32[]{:S(2)}, u32[]{:S(2)}) collective-permute-start(bf16[128,512]{1,0:T(8,128)(2,1)S(1)} %shard_map.90), channel_id=1, source_target_pairs={{0,248},{4,252},{8,192},{12,196},{16,200},{20,204},{24,208},{28,21... | collective-permute-start | bytes 393224 | tf_op jit(solution)/shard_map/ppermute | solution.py:337
  75.4 6.6 %collective-permute-start.8 = (bf16[128,512]{1,0:T(8,128)(2,1)S(1)}, bf16[128,512]{1,0:T(8,128)(2,1)S(1)}, u32[]{:S(2)}, u32[]{:S(2)}) collective-permute-start(bf16[128,512]{1,0:T(8,128)(2,1)S(1)} %shard_map.90), channel_id=1, source_target_pairs={{0,192},{4,196},{8,200},{12,204},{16,208},{20,212},{24,216},{28,22... | collective-permute-start | bytes 393224 | tf_op jit(solution)/shard_map/ppermute | solution.py:337
  82.0 2.0 %collective-permute-start.10 = (bf16[128,512]{1,0:T(8,128)(2,1)S(1)}, bf16[128,512]{1,0:T(8,128)(2,1)S(1)}, u32[]{:S(2)}, u32[]{:S(2)}) collective-permute-start(bf16[128,512]{1,0:T(8,128)(2,1)S(1)} %shard_map.91), channel_id=1, source_target_pairs={{0,4},{4,0},{8,12},{12,8},{16,20},{20,16},{24,28},{28,24},{32,36},... | collective-permute-start | bytes 393224 | tf_op jit(solution)/shard_map/ppermute | solution.py:384
  103.5 6.0 %collective-permute-start.19 = (bf16[16,8,384]{2,1,0:T(8,128)(2,1)S(1)}, bf16[16,8,384]{2,1,0:T(8,128)(2,1)S(1)}, u32[]{:S(2)}, u32[]{:S(2)}) collective-permute-start(bf16[16,8,384]{2,1,0:T(8,128)(2,1)S(1)} %get-tuple-element.32), channel_id=1, source_target_pairs={{0,1},{1,2},{2,3},{3,0},{4,5},{5,6},{6,7},{7,4},{8,9},{9,10},{10,1... | collective-permute-start | bytes 294920 | tf_op jit(solution)/shard_map/ppermute | solution.py:341
  104.8 7.8 %collective-permute-start.20 = (bf16[16,8,384]{2,1,0:T(8,128)(2,1)S(1)}, bf16[16,8,384]{2,1,0:T(8,128)(2,1)S(1)}, u32[]{:S(2)}, u32[]{:S(2)}) collective-permute-start(bf16[16,8,384]{2,1,0:T(8,128)(2,1)S(1)} %get-tuple-element.33), channel_id=1, source_target_pairs={{0,2},{1,3},{2,0},{3,1},{4,6},{5,7},{6,4},{7,5},{8,10},{9,11},{10,... | collective-permute-start | bytes 294920 | tf_op jit(solution)/shard_map/ppermute | solution.py:341
  107.2 5.3 %collective-permute-start.21 = (bf16[16,8,384]{2,1,0:T(8,128)(2,1)S(1)}, bf16[16,8,384]{2,1,0:T(8,128)(2,1)S(1)}, u32[]{:S(2)}, u32[]{:S(2)}) collective-permute-start(bf16[16,8,384]{2,1,0:T(8,128)(2,1)S(1)} %get-tuple-element.34), channel_id=1, source_target_pairs={{0,3},{1,0},{2,1},{3,2},{4,7},{5,4},{6,5},{7,6},{8,11},{9,8},{10,9... | collective-permute-start | bytes 294920 | tf_op jit(solution)/shard_map/ppermute | solution.py:341
  124.0 4.7 %collective-permute-start.24 = (bf16[16,8,384]{2,1,0:T(8,128)(2,1)S(1)}, bf16[16,8,384]{2,1,0:T(8,128)(2,1)S(1)}, u32[]{:S(2)}, u32[]{:S(2)}) collective-permute-start(bf16[16,8,384]{2,1,0:T(8,128)(2,1)S(1)} %all_to_all.11.refs_0_), channel_id=1, source_target_pairs={{0,3},{1,0},{2,1},{3,2},{4,7},{5,4},{6,5},{7,6},{8,11},{9,8},{10,9... | collective-permute-start | bytes 294920 | tf_op jit(solution)/shard_map/ppermute | solution.py:341
  126.1 5.6 %collective-permute-start.23 = (bf16[16,8,384]{2,1,0:T(8,128)(2,1)S(1)}, bf16[16,8,384]{2,1,0:T(8,128)(2,1)S(1)}, u32[]{:S(2)}, u32[]{:S(2)}) collective-permute-start(bf16[16,8,384]{2,1,0:T(8,128)(2,1)S(1)} %all_to_all.11.refs_0_), channel_id=1, source_target_pairs={{0,2},{1,3},{2,0},{3,1},{4,6},{5,7},{6,4},{7,5},{8,10},{9,11},{10,... | collective-permute-start | bytes 294920 | tf_op jit(solution)/shard_map/ppermute | solution.py:341
  126.8 7.5 %collective-permute-start.22 = (bf16[16,8,384]{2,1,0:T(8,128)(2,1)S(1)}, bf16[16,8,384]{2,1,0:T(8,128)(2,1)S(1)}, u32[]{:S(2)}, u32[]{:S(2)}) collective-permute-start(bf16[16,8,384]{2,1,0:T(8,128)(2,1)S(1)} %all_to_all.11.refs_0_), channel_id=1, source_target_pairs={{0,1},{1,2},{2,3},{3,0},{4,5},{5,6},{6,7},{7,4},{8,9},{9,10},{10,1... | collective-permute-start | bytes 294920 | tf_op jit(solution)/shard_map/ppermute | solution.py:341

commit v2 on v1

--- a/solution.py
+++ b/solution.py
@@ -297,36 +297,47 @@
     )(late, *ring, swapped)
 
 
-def assemble_kernel(*refs):
-    parts, (spatial_ref, temporal_ref) = refs[:CLIPS], refs[CLIPS:]
+def assemble_kernel(sources, kept, *refs):
+    parts = refs[: len(sources)]
+    spatial_ref, temporal_ref, lines, sems = refs[len(sources) + kept :]
     d = lax.axis_index("dp")
-    for k in range(CLIPS):
+    copies = []
+    for i, k in enumerate(sources):
         source = lax.rem(d + CLIPS - k, CLIPS)
         rows = pl.ds(pl.multiple_of(source * SUB, SUB), SUB)
-        part = parts[k][...].astype(F32)
+        part = parts[i][...].astype(F32)
         for tap in range(TAPS):
-            line = jnp.concatenate(
+            lines[i, tap] = jnp.concatenate(
                 [part[s, :, tap * SLICE : (tap + 1) * SLICE] for s in range(FRAMES)], axis=-1
             )
-            if tap < 9:
-                spatial_ref[tap, rows, :] = line
-            else:
-                temporal_ref[tap - 9, rows, :] = line
-
-
-def assemble(parts):
-    return pl.pallas_call(
-        assemble_kernel,
-        name="assemble",
+        for j, (first, size, out) in enumerate(((0, 9, spatial_ref), (9, 3, temporal_ref))):
+            c = pltpu.make_async_copy(
+                lines.at[i, pl.ds(first, size)], out.at[:, rows, :], sems.at[i, j]
+            )
+            c.start()
+            copies.append(c)
+    for c in copies:
+        c.wait()
+
+
+def assemble(sources, parts, outs=()):
+    n = len(sources)
+    return pl.pallas_call(
+        functools.partial(assemble_kernel, sources, len(outs)),
         out_shape=(
             jax.ShapeDtypeStruct((9, SLICE, CH), F32),
             jax.ShapeDtypeStruct((3, SLICE, CH), F32),
         ),
-        in_specs=[VMEM] * CLIPS,
-        out_specs=(VMEM, VMEM),
-        compiler_params=pltpu.CompilerParams(vmem_limit_bytes=24 << 20),
-        cost_estimate=pl.CostEstimate(flops=1000000, bytes_accessed=1200000, transcendentals=0),
-    )(*parts)
+        in_specs=[VMEM] * n + [ANY] * len(outs),
+        out_specs=(ANY, ANY),
+        scratch_shapes=[
+            pltpu.VMEM((n, TAPS, SUB, CH), F32),
+            pltpu.SemaphoreType.DMA((n, 2)),
+        ],
+        input_output_aliases={n + i: i for i in range(len(outs))},
+        compiler_params=pltpu.CompilerParams(vmem_limit_bytes=8 << 20),
+        cost_estimate=pl.CostEstimate(flops=1000000, bytes_accessed=300000 * n, transcendentals=0),
+    )(*parts, *outs)
 
 
 def send(value, axes, sizes, step):
@@ -351,12 +362,11 @@
     x = section_inputs.reshape(CELLS, CH)
     ws, wt = w_spatial[0], w_temporal[0]
     cot = grad_output.reshape(CELLS, CH)
-    zeros = lead()
+    start, count, zeros = lax.optimization_barrier((frame_start, frame_count, lead()))
+    keep = keep_of(start, count, zeros)
     ahead2 = send(cot, axes, sizes, (0, -2))
     ahead1 = send(cot, axes, sizes, (0, -1))
     mine, slope, wtt, wst, cot = forward(x, wt, ws, cot)
-    start, count, slope = lax.optimization_barrier((frame_start, frame_count, slope))
-    keep = keep_of(start, count, zeros)
     head = [keep, cot, ahead1, ahead2]
     head_specs = [VMEM] * 4
     ring = {0: mine}
@@ -405,7 +415,8 @@
     share = sum(s.astype(F32) for s in shares).astype(BF16)
     share = lax.all_to_all(share, "seq", 0, 0, tiled=True)
     parts = [share] + [around(share, "dp", CLIPS, k) for k in (1, 2, 3)]
-    spatial, temporal = assemble(parts)
+    outs = assemble((0, 3, 2), [parts[k] for k in (0, 3, 2)])
+    spatial, temporal = assemble((1,), [parts[1]], outs)
     return grad_in.reshape(section_inputs.shape), spatial[None], temporal[None]
 
 

time: 136 us -> 134 us (0.985)
  the two profiles are of different devices: /device:TPU:1 before, /device:TPU:27 now
where the time goes in v2:
time: 134 us
  waiting for transfers between devices  53.4 us (40%)
  starting transfers between devices  33.3 us (25%)
  blocking collectives  28.8 us (21%)
  Pallas kernels  11.7 us (9%)
  local copies, waits for them, and re-layouts  4.64 us (3%)
  between operations  2.28 us (2%)
    ppermute x8, waiting for transfers between devices, send(): return lax.ppermute(value, axes, pairs)  26.7 us
    ppermute x13, waiting for transfers between devices, around(): lax.ppermute(value, axis, [(i, (i + step) % size) for i in range(size)])  23.7 us
    ppermute x13, starting transfers between devices, around(): lax.ppermute(value, axis, [(i, (i + step) % size) for i in range(size)])  18.1 us
    all_to_all x1, blocking collectives, backward(): gathered = lax.all_to_all(late, 'seq', 0, 0, tiled=True)  16.8 us
    all_to_all x1, blocking collectives, backward(): share = lax.all_to_all(share, 'seq', 0, 0, tiled=True)  12 us
    ppermute x8, starting transfers between devices, send(): return lax.ppermute(value, axes, pairs)  7.6 us
    pallas_call x8, Pallas kernels, small(): pl.pallas_call(kernel, out_shape=tuple((jax.ShapeDtypeStruct(o, BF16) for...  5.54 us
    unnamed x8, local copies, waits for them, and re-layouts  4.64 us
  transfers between devices with their start and end apart: 25, of which 18 were waited for; matrix products, arithmetic and copies ran while one was open for 0% of the time, Pallas kernels for 5%

profile of v2, /device:TPU:27, one launch (start us, length us, event | category | flops | bytes accessed | tf_op | source)
XLA Modules:
  0.0 134.1 jit_solution(3390851957425078188)
XLA Ops:
  0.6 2.3 %copy-done = bf16[1,9,512,512]{3,2,1,0:T(8,128)(2,1)S(1)} copy-done((bf16[1,9,512,512]{3,2,1,0:T(8,128)(2,1)S(1)}, bf16[1,9,512,512]{3,2,1,0:T(8,128)(2,1)}, u32[]{:S(2)}) %copy-start) | copy-done | bytes 4718616
  3.0 1.4 %copy-done.1 = bf16[1,3,512,512]{3,2,1,0:T(8,128)(2,1)S(1)} copy-done((bf16[1,3,512,512]{3,2,1,0:T(8,128)(2,1)S(1)}, bf16[1,3,512,512]{3,2,1,0:T(8,128)(2,1)}, u32[]{:S(2)}) %copy-start.1) | copy-done | bytes 1572888
  5.3 1.8 %block_forward.1 = (bf16[2,512,128]{2,1,0:T(8,128)(2,1)S(1)}, f32[128,512]{1,0:T(8,128)S(1)}, bf16[3,512,512]{2,1,0:T(8,128)(2,1)S(1)}, bf16[9,512,512]{2,1,0:T(8,128)(2,1)S(1)}, bf16[128,512]{1,0:T(8,128)(2,1)S(1)}) custom-call(bf16[128,512]{1,0:T(8,128)(2,1)S(1)} %bitcast.9, bf16[3,512,512]{2,1,0:T(8,128)(2,1)S(1)} %bitcast.8, ...), custom_call_target="tpu_custom_call" | custom-call | flops 1208000000 | bytes 13000000 | tf_op jit(solution)/shard_map/block_forward/pallas_call | solution.py:111
  7.1 1.7 %collective-permute-start.14 = (bf16[2,512,128]{2,1,0:T(8,128)(2,1)S(1)}, bf16[2,512,128]{2,1,0:T(8,128)(2,1)S(1)}, u32[]{:S(2)}, u32[]{:S(2)}) collective-permute-start(bf16[2,512,128]{2,1,0:T(8,128)(2,1)S(1)} %get-tuple-element.32.refs_0_), channel_id=1, source_target_pairs={{0,8},{4,12},{8,16},{12,20},{16,24},{20,28},{24,32},{28,36},{32,40... | collective-permute-start | bytes 786440 | tf_op jit(solution)/shard_map/ppermute | solution.py:352
  8.8 4.0 %collective-permute-start.11 = (bf16[2,512,128]{2,1,0:T(8,128)(2,1)S(1)}, bf16[2,512,128]{2,1,0:T(8,128)(2,1)S(1)}, u32[]{:S(2)}, u32[]{:S(2)}) collective-permute-start(bf16[2,512,128]{2,1,0:T(8,128)(2,1)S(1)} %get-tuple-element.32.refs_0_), channel_id=1, source_target_pairs={{0,56},{4,60},{8,0},{12,4},{16,8},{20,12},{24,16},{28,20},{32,24},... | collective-permute-start | bytes 786440 | tf_op jit(solution)/shard_map/ppermute | solution.py:352
  12.9 5.9 %collective-permute-done.14.refs_7_ = bf16[2,512,128]{2,1,0:T(8,128)(2,1)S(1)} collective-permute-done((bf16[2,512,128]{2,1,0:T(8,128)(2,1)S(1)}, bf16[2,512,128]{2,1,0:T(8,128)(2,1)S(1)}, u32[]{:S(2)}, u32[]{:S(2)}) %collective-permute-start.14) | collective-permute-done | bytes 262176 | tf_op jit(solution)/shard_map/ppermute | solution.py:352
  18.8 2.7 %collective-permute-start.12 = (bf16[2,512,128]{2,1,0:T(8,128)(2,1)S(1)}, bf16[2,512,128]{2,1,0:T(8,128)(2,1)S(1)}, u32[]{:S(2)}, u32[]{:S(2)}) collective-permute-start(bf16[2,512,128]{2,1,0:T(8,128)(2,1)S(1)} %collective-permute-done.11.refs_1_), channel_id=1, source_target_pairs={{0,56},{4,60},{8,0},{12,4},{16,8},{20,12},{24,16},{28,20},{32,24},... | collective-permute-start | bytes 786440 | tf_op jit(solution)/shard_map/ppermute | solution.py:352
  21.5 5.1 %collective-permute-done.15.refs_6_ = bf16[2,512,128]{2,1,0:T(8,128)(2,1)S(1)} collective-permute-done((bf16[2,512,128]{2,1,0:T(8,128)(2,1)S(1)}, bf16[2,512,128]{2,1,0:T(8,128)(2,1)S(1)}, u32[]{:S(2)}, u32[]{:S(2)}) %collective-permute-start.15) | collective-permute-done | bytes 262176 | tf_op jit(solution)/shard_map/ppermute | solution.py:352
  26.6 2.7 %collective-permute-start.13 = (bf16[2,512,128]{2,1,0:T(8,128)(2,1)S(1)}, bf16[2,512,128]{2,1,0:T(8,128)(2,1)S(1)}, u32[]{:S(2)}, u32[]{:S(2)}) collective-permute-start(bf16[2,512,128]{2,1,0:T(8,128)(2,1)S(1)} %collective-permute-done.12.refs_2_), channel_id=1, source_target_pairs={{0,56},{4,60},{8,0},{12,4},{16,8},{20,12},{24,16},{28,20},{32,24},... | collective-permute-start | bytes 786440 | tf_op jit(solution)/shard_map/ppermute | solution.py:352
  29.3 4.3 %collective-permute-done.16.refs_5_ = bf16[2,512,128]{2,1,0:T(8,128)(2,1)S(1)} collective-permute-done((bf16[2,512,128]{2,1,0:T(8,128)(2,1)S(1)}, bf16[2,512,128]{2,1,0:T(8,128)(2,1)S(1)}, u32[]{:S(2)}, u32[]{:S(2)}) %collective-permute-start.16) | collective-permute-done | bytes 262176 | tf_op jit(solution)/shard_map/ppermute | solution.py:352
  33.6 2.7 %collective-permute-start.1 = (bf16[128,512]{1,0:T(8,128)(2,1)S(1)}, bf16[128,512]{1,0:T(8,128)(2,1)S(1)}, u32[]{:S(2)}, u32[]{:S(2)}) collective-permute-start(bf16[128,512]{1,0:T(8,128)(2,1)S(1)} %bitcast.13), channel_id=1, source_target_pairs={{0,56},{4,60},{8,0},{12,4},{16,8},{20,12},{24,16},{28,20},{32,24},... | collective-permute-start | bytes 393224 | tf_op jit(solution)/shard_map/ppermute | solution.py:348
  36.2 3.5 %collective-permute-start = (bf16[128,512]{1,0:T(8,128)(2,1)S(1)}, bf16[128,512]{1,0:T(8,128)(2,1)S(1)}, u32[]{:S(2)}, u32[]{:S(2)}) collective-permute-start(bf16[128,512]{1,0:T(8,128)(2,1)S(1)} %bitcast.14), channel_id=1, source_target_pairs={{0,60},{4,0},{8,4},{12,8},{16,12},{20,16},{24,20},{28,24},{32,28},... | collective-permute-start | bytes 393224 | tf_op jit(solution)/shard_map/ppermute | solution.py:348
  40.2 4.2 %collective-permute-start.18 = (bf16[8,2,512,128]{3,2,1,0:T(8,128)(2,1)S(1)}, bf16[8,2,512,128]{3,2,1,0:T(8,128)(2,1)S(1)}, u32[]{:S(2)}, u32[]{:S(2)}) collective-permute-start(bf16[8,2,512,128]{3,2,1,0:T(8,128)(2,1)S(1)} %pack.1), channel_id=1, source_target_pairs={{0,4},{4,0},{8,12},{12,8},{16,20},{20,16},{24,28},{28,24},{32,36},... | collective-permute-start | bytes 6291464 | tf_op jit(solution)/shard_map/ppermute | solution.py:409
  48.0 6.2 %collective-permute-done.3.two_ref.refs_6_ = bf16[128,512]{1,0:T(8,128)(2,1)S(1)} collective-permute-done((bf16[128,512]{1,0:T(8,128)(2,1)S(1)}, bf16[128,512]{1,0:T(8,128)(2,1)S(1)}, u32[]{:S(2)}, u32[]{:S(2)}) %collective-permute-start.3) | collective-permute-done | bytes 131104 | tf_op jit(solution)/shard_map/ppermute | solution.py:348
  54.2 3.1 %collective-permute-done.2.none_ref.refs_4_ = bf16[128,512]{1,0:T(8,128)(2,1)S(1)} collective-permute-done((bf16[128,512]{1,0:T(8,128)(2,1)S(1)}, bf16[128,512]{1,0:T(8,128)(2,1)S(1)}, u32[]{:S(2)}, u32[]{:S(2)}) %collective-permute-start.2) | collective-permute-done | bytes 131104 | tf_op jit(solution)/shard_map/ppermute | solution.py:348
  60.4 6.7 %collective-permute-done.6.two_ref.refs_6_ = bf16[128,512]{1,0:T(8,128)(2,1)S(1)} collective-permute-done((bf16[128,512]{1,0:T(8,128)(2,1)S(1)}, bf16[128,512]{1,0:T(8,128)(2,1)S(1)}, u32[]{:S(2)}, u32[]{:S(2)}) %collective-permute-start.6) | collective-permute-done | bytes 131104 | tf_op jit(solution)/shard_map/ppermute | solution.py:348
  67.2 2.0 %collective-permute-done.5.none_ref.refs_4_ = bf16[128,512]{1,0:T(8,128)(2,1)S(1)} collective-permute-done((bf16[128,512]{1,0:T(8,128)(2,1)S(1)}, bf16[128,512]{1,0:T(8,128)(2,1)S(1)}, u32[]{:S(2)}, u32[]{:S(2)}) %collective-permute-start.5) | collective-permute-done | bytes 131104 | tf_op jit(solution)/shard_map/ppermute | solution.py:348
  69.1 1.3 collective-permute-start.7
  72.8 6.7 %collective-permute-done.9.two_ref.refs_6_ = bf16[128,512]{1,0:T(8,128)(2,1)S(1)} collective-permute-done((bf16[128,512]{1,0:T(8,128)(2,1)S(1)}, bf16[128,512]{1,0:T(8,128)(2,1)S(1)}, u32[]{:S(2)}, u32[]{:S(2)}) %collective-permute-start.9) | collective-permute-done | bytes 131104 | tf_op jit(solution)/shard_map/ppermute | solution.py:348
  79.5 2.0 %collective-permute-done.8.none_ref.refs_4_ = bf16[128,512]{1,0:T(8,128)(2,1)S(1)} collective-permute-done((bf16[128,512]{1,0:T(8,128)(2,1)S(1)}, bf16[128,512]{1,0:T(8,128)(2,1)S(1)}, u32[]{:S(2)}, u32[]{:S(2)}) %collective-permute-start.8) | collective-permute-done | bytes 131104 | tf_op jit(solution)/shard_map/ppermute | solution.py:348
  81.5 1.3 collective-permute-start.10
  84.3 16.8 %all_to_all.10.late_ref = bf16[16,64,128]{2,1,0:T(8,128)(2,1)S(1)} all-to-all(bf16[16,64,128]{2,1,0:T(8,128)(2,1)S(1)} %get-tuple-element.31), channel_id=1, replica_groups=mesh['pipe'=4,'seq'=16,'dp'=4] {'seq'}, dimensions={0} | all-to-all | bytes 524288 | tf_op jit(solution)/shard_map/all_to_all | solution.py:406
  101.1 2.2 %weight_grads.1 = (bf16[16,8,384]{2,1,0:T(8,128)(2,1)S(1)}, bf16[16,8,384]{2,1,0:T(8,128)(2,1)S(1)}, bf16[16,8,384]{2,1,0:T(8,128)(2,1)S(1)}, bf16[16,8,384]{2,1,0:T(8,128)(2,1)S(1)}) custom-call(bf16[16,64,128]{2,1,0:T(8,128)(2,1)S(1)} %all_to_all.10.late_ref, bf16[2,512,128]{2,1,0:T(8,128)(2,1)S(1)} %get-tuple-element.32.refs_0_, ...), custom_call_target="tpu_custom_call" | custom-call | flops 1610000000 | bytes 5000000 | tf_op jit(solution)/shard_map/weight_grads/pallas_call | solution.py:285
  103.4 1.3 collective-permute-start.19
  105.4 1.9 %collective-permute-start.21 = (bf16[16,8,384]{2,1,0:T(8,128)(2,1)S(1)}, bf16[16,8,384]{2,1,0:T(8,128)(2,1)S(1)}, u32[]{:S(2)}, u32[]{:S(2)}) collective-permute-start(bf16[16,8,384]{2,1,0:T(8,128)(2,1)S(1)} %get-tuple-element.36), channel_id=1, source_target_pairs={{0,3},{1,0},{2,1},{3,2},{4,7},{5,4},{6,5},{7,6},{8,11},{9,8},{10,9... | collective-permute-start | bytes 294920 | tf_op jit(solution)/shard_map/ppermute | solution.py:352
  108.1 2.5 %collective-permute-done.20 = bf16[16,8,384]{2,1,0:T(8,128)(2,1)S(1)} collective-permute-done((bf16[16,8,384]{2,1,0:T(8,128)(2,1)S(1)}, bf16[16,8,384]{2,1,0:T(8,128)(2,1)S(1)}, u32[]{:S(2)}, u32[]{:S(2)}) %collective-permute-start.20) | collective-permute-done | bytes 98336 | tf_op jit(solution)/shard_map/ppermute | solution.py:352
  111.7 12.0 %all_to_all.11.refs_0_ = bf16[16,8,384]{2,1,0:T(8,128)(2,1)S(1)} all-to-all(bf16[16,8,384]{2,1,0:T(8,128)(2,1)S(1)} %add_convert_fusion), channel_id=1, replica_groups=mesh['pipe'=4,'seq'=16,'dp'=4] {'seq'}, dimensions={0} | all-to-all | bytes 196608 | tf_op jit(solution)/shard_map/all_to_all | solution.py:416
  123.7 1.6 %collective-permute-start.24 = (bf16[16,8,384]{2,1,0:T(8,128)(2,1)S(1)}, bf16[16,8,384]{2,1,0:T(8,128)(2,1)S(1)}, u32[]{:S(2)}, u32[]{:S(2)}) collective-permute-start(bf16[16,8,384]{2,1,0:T(8,128)(2,1)S(1)} %all_to_all.11.refs_0_), channel_id=1, source_target_pairs={{0,2},{1,3},{2,0},{3,1},{4,6},{5,7},{6,4},{7,5},{8,10},{9,11},{10,... | collective-permute-start | bytes 294920 | tf_op jit(solution)/shard_map/ppermute | solution.py:352
  125.3 1.2 collective-permute-start.23
  126.8 1.4 %shard_map.93 = bf16[128,512]{1,0:T(8,128)(2,1)} custom-call(bf16[128,512]{1,0:T(8,128)(2,1)S(1)} %get-tuple-element.29.cot_ref, bf16[128,512]{1,0:T(8,128)(2,1)S(1)} %get-tuple-element.30.pre_ref, bf16[9,512,512]{2,1,0:T(8,128)(2,1)S(1)} %get-tuple-element.28.refs_6_.refs_9_.wst_ref), custom_call_target="tpu_custom_call" | custom-call | flops 604000000 | bytes 5000000 | tf_op jit(solution)/shard_map/pallas_call | solution.py:184
  128.2 1.4 %collective-permute-done.24.refs_2_ = bf16[16,8,384]{2,1,0:T(8,128)(2,1)S(1)} collective-permute-done((bf16[16,8,384]{2,1,0:T(8,128)(2,1)S(1)}, bf16[16,8,384]{2,1,0:T(8,128)(2,1)S(1)}, u32[]{:S(2)}, u32[]{:S(2)}) %collective-permute-start.24) | collective-permute-done | bytes 98336 | tf_op jit(solution)/shard_map/ppermute | solution.py:352
  129.6 2.4 %collective-permute-done.23.refs_1_ = bf16[16,8,384]{2,1,0:T(8,128)(2,1)S(1)} collective-permute-done((bf16[16,8,384]{2,1,0:T(8,128)(2,1)S(1)}, bf16[16,8,384]{2,1,0:T(8,128)(2,1)S(1)}, u32[]{:S(2)}, u32[]{:S(2)}) %collective-permute-start.23) | collective-permute-done | bytes 98336 | tf_op jit(solution)/shard_map/ppermute | solution.py:352
  (45 shorter events, 15.3 us)
Async XLA Ops:
  0.6 2.3 %copy-start = (bf16[1,9,512,512]{3,2,1,0:T(8,128)(2,1)S(1)}, bf16[1,9,512,512]{3,2,1,0:T(8,128)(2,1)}, u32[]{:S(2)}) copy-start(bf16[1,9,512,512]{3,2,1,0:T(8,128)(2,1)} %param.7) | copy-start | bytes 14155780
  3.0 1.4 %copy-start.1 = (bf16[1,3,512,512]{3,2,1,0:T(8,128)(2,1)S(1)}, bf16[1,3,512,512]{3,2,1,0:T(8,128)(2,1)}, u32[]{:S(2)}) copy-start(bf16[1,3,512,512]{3,2,1,0:T(8,128)(2,1)} %param.8) | copy-start | bytes 4718596
  4.4 0.9 copy-start.2
  5.3 28.3 %copy-start.3 = (bf16[1,1,16,8,512]{4,3,2,1,0:T(8,128)(2,1)S(1)}, bf16[1,1,16,8,512]{4,3,2,1,0:T(8,128)(2,1)}, u32[]{:S(2)}) copy-start(bf16[1,1,16,8,512]{4,3,2,1,0:T(8,128)(2,1)} %param.9) | copy-start | bytes 393220
  7.1 11.7 %collective-permute-start.14 = (bf16[2,512,128]{2,1,0:T(8,128)(2,1)S(1)}, bf16[2,512,128]{2,1,0:T(8,128)(2,1)S(1)}, u32[]{:S(2)}, u32[]{:S(2)}) collective-permute-start(bf16[2,512,128]{2,1,0:T(8,128)(2,1)S(1)} %get-tuple-element.32.refs_0_), channel_id=1, source_target_pairs={{0,8},{4,12},{8,16},{12,20},{16,24},{20,28},{24,32},{28,36},{32,40... | collective-permute-start | bytes 786440 | tf_op jit(solution)/shard_map/ppermute | solution.py:352
  8.8 9.9 %collective-permute-start.11 = (bf16[2,512,128]{2,1,0:T(8,128)(2,1)S(1)}, bf16[2,512,128]{2,1,0:T(8,128)(2,1)S(1)}, u32[]{:S(2)}, u32[]{:S(2)}) collective-permute-start(bf16[2,512,128]{2,1,0:T(8,128)(2,1)S(1)} %get-tuple-element.32.refs_0_), channel_id=1, source_target_pairs={{0,56},{4,60},{8,0},{12,4},{16,8},{20,12},{24,16},{28,20},{32,24},... | collective-permute-start | bytes 786440 | tf_op jit(solution)/shard_map/ppermute | solution.py:352
  18.8 7.8 %collective-permute-start.15 = (bf16[2,512,128]{2,1,0:T(8,128)(2,1)S(1)}, bf16[2,512,128]{2,1,0:T(8,128)(2,1)S(1)}, u32[]{:S(2)}, u32[]{:S(2)}) collective-permute-start(bf16[2,512,128]{2,1,0:T(8,128)(2,1)S(1)} %collective-permute-done.14.refs_7_), channel_id=1, source_target_pairs={{0,8},{4,12},{8,16},{12,20},{16,24},{20,28},{24,32},{28,36},{32,40... | collective-permute-start | bytes 786440 | tf_op jit(solution)/shard_map/ppermute | solution.py:352
  18.8 7.8 %collective-permute-start.12 = (bf16[2,512,128]{2,1,0:T(8,128)(2,1)S(1)}, bf16[2,512,128]{2,1,0:T(8,128)(2,1)S(1)}, u32[]{:S(2)}, u32[]{:S(2)}) collective-permute-start(bf16[2,512,128]{2,1,0:T(8,128)(2,1)S(1)} %collective-permute-done.11.refs_1_), channel_id=1, source_target_pairs={{0,56},{4,60},{8,0},{12,4},{16,8},{20,12},{24,16},{28,20},{32,24},... | collective-permute-start | bytes 786440 | tf_op jit(solution)/shard_map/ppermute | solution.py:352
  26.6 7.0 %collective-permute-start.16 = (bf16[2,512,128]{2,1,0:T(8,128)(2,1)S(1)}, bf16[2,512,128]{2,1,0:T(8,128)(2,1)S(1)}, u32[]{:S(2)}, u32[]{:S(2)}) collective-permute-start(bf16[2,512,128]{2,1,0:T(8,128)(2,1)S(1)} %collective-permute-done.15.refs_6_), channel_id=1, source_target_pairs={{0,8},{4,12},{8,16},{12,20},{16,24},{20,28},{24,32},{28,36},{32,40... | collective-permute-start | bytes 786440 | tf_op jit(solution)/shard_map/ppermute | solution.py:352
  26.6 13.2 %collective-permute-start.13 = (bf16[2,512,128]{2,1,0:T(8,128)(2,1)S(1)}, bf16[2,512,128]{2,1,0:T(8,128)(2,1)S(1)}, u32[]{:S(2)}, u32[]{:S(2)}) collective-permute-start(bf16[2,512,128]{2,1,0:T(8,128)(2,1)S(1)} %collective-permute-done.12.refs_2_), channel_id=1, source_target_pairs={{0,56},{4,60},{8,0},{12,4},{16,8},{20,12},{24,16},{28,20},{32,24},... | collective-permute-start | bytes 786440 | tf_op jit(solution)/shard_map/ppermute | solution.py:352
  33.6 6.4 %collective-permute-start.17 = (bf16[2,512,128]{2,1,0:T(8,128)(2,1)S(1)}, bf16[2,512,128]{2,1,0:T(8,128)(2,1)S(1)}, u32[]{:S(2)}, u32[]{:S(2)}) collective-permute-start(bf16[2,512,128]{2,1,0:T(8,128)(2,1)S(1)} %collective-permute-done.16.refs_5_), channel_id=1, source_target_pairs={{0,8},{4,12},{8,16},{12,20},{16,24},{20,28},{24,32},{28,36},{32,40... | collective-permute-start | bytes 786440 | tf_op jit(solution)/shard_map/ppermute | solution.py:352
  33.6 12.2 %collective-permute-start.1 = (bf16[128,512]{1,0:T(8,128)(2,1)S(1)}, bf16[128,512]{1,0:T(8,128)(2,1)S(1)}, u32[]{:S(2)}, u32[]{:S(2)}) collective-permute-start(bf16[128,512]{1,0:T(8,128)(2,1)S(1)} %bitcast.13), channel_id=1, source_target_pairs={{0,56},{4,60},{8,0},{12,4},{16,8},{20,12},{24,16},{28,20},{32,24},... | collective-permute-start | bytes 393224 | tf_op jit(solution)/shard_map/ppermute | solution.py:348
  36.2 9.5 %collective-permute-start = (bf16[128,512]{1,0:T(8,128)(2,1)S(1)}, bf16[128,512]{1,0:T(8,128)(2,1)S(1)}, u32[]{:S(2)}, u32[]{:S(2)}) collective-permute-start(bf16[128,512]{1,0:T(8,128)(2,1)S(1)} %bitcast.14), channel_id=1, source_target_pairs={{0,60},{4,0},{8,4},{12,8},{16,12},{20,16},{24,20},{28,24},{32,28},... | collective-permute-start | bytes 393224 | tf_op jit(solution)/shard_map/ppermute | solution.py:348
  40.2 60.9 %collective-permute-start.18 = (bf16[8,2,512,128]{3,2,1,0:T(8,128)(2,1)S(1)}, bf16[8,2,512,128]{3,2,1,0:T(8,128)(2,1)S(1)}, u32[]{:S(2)}, u32[]{:S(2)}) collective-permute-start(bf16[8,2,512,128]{3,2,1,0:T(8,128)(2,1)S(1)} %pack.1), channel_id=1, source_target_pairs={{0,4},{4,0},{8,12},{12,8},{16,20},{20,16},{24,28},{28,24},{32,36},... | collective-permute-start | bytes 6291464 | tf_op jit(solution)/shard_map/ppermute | solution.py:409
  46.9 7.3 %collective-permute-start.3 = (bf16[128,512]{1,0:T(8,128)(2,1)S(1)}, bf16[128,512]{1,0:T(8,128)(2,1)S(1)}, u32[]{:S(2)}, u32[]{:S(2)}) collective-permute-start(bf16[128,512]{1,0:T(8,128)(2,1)S(1)} %shard_map.86), channel_id=1, source_target_pairs={{0,248},{4,252},{8,192},{12,196},{16,200},{20,204},{24,208},{28,21... | collective-permute-start | bytes 393224 | tf_op jit(solution)/shard_map/ppermute | solution.py:348
  47.8 9.5 %collective-permute-start.2 = (bf16[128,512]{1,0:T(8,128)(2,1)S(1)}, bf16[128,512]{1,0:T(8,128)(2,1)S(1)}, u32[]{:S(2)}, u32[]{:S(2)}) collective-permute-start(bf16[128,512]{1,0:T(8,128)(2,1)S(1)} %shard_map.86), channel_id=1, source_target_pairs={{0,192},{4,196},{8,200},{12,204},{16,208},{20,212},{24,216},{28,22... | collective-permute-start | bytes 393224 | tf_op jit(solution)/shard_map/ppermute | solution.py:348
  57.3 1.7 %collective-permute-start.4 = (bf16[128,512]{1,0:T(8,128)(2,1)S(1)}, bf16[128,512]{1,0:T(8,128)(2,1)S(1)}, u32[]{:S(2)}, u32[]{:S(2)}) collective-permute-start(bf16[128,512]{1,0:T(8,128)(2,1)S(1)} %shard_map.87), channel_id=1, source_target_pairs={{0,4},{4,0},{8,12},{12,8},{16,20},{20,16},{24,28},{28,24},{32,36},... | collective-permute-start | bytes 393224 | tf_op jit(solution)/shard_map/ppermute | solution.py:394
  60.2 6.9 %collective-permute-start.6 = (bf16[128,512]{1,0:T(8,128)(2,1)S(1)}, bf16[128,512]{1,0:T(8,128)(2,1)S(1)}, u32[]{:S(2)}, u32[]{:S(2)}) collective-permute-start(bf16[128,512]{1,0:T(8,128)(2,1)S(1)} %shard_map.88), channel_id=1, source_target_pairs={{0,248},{4,252},{8,192},{12,196},{16,200},{20,204},{24,208},{28,21... | collective-permute-start | bytes 393224 | tf_op jit(solution)/shard_map/ppermute | solution.py:348
  60.3 8.8 %collective-permute-start.5 = (bf16[128,512]{1,0:T(8,128)(2,1)S(1)}, bf16[128,512]{1,0:T(8,128)(2,1)S(1)}, u32[]{:S(2)}, u32[]{:S(2)}) collective-permute-start(bf16[128,512]{1,0:T(8,128)(2,1)S(1)} %shard_map.88), channel_id=1, source_target_pairs={{0,192},{4,196},{8,200},{12,204},{16,208},{20,212},{24,216},{28,22... | collective-permute-start | bytes 393224 | tf_op jit(solution)/shard_map/ppermute | solution.py:348
  69.1 2.3 %collective-permute-start.7 = (bf16[128,512]{1,0:T(8,128)(2,1)S(1)}, bf16[128,512]{1,0:T(8,128)(2,1)S(1)}, u32[]{:S(2)}, u32[]{:S(2)}) collective-permute-start(bf16[128,512]{1,0:T(8,128)(2,1)S(1)} %shard_map.89), channel_id=1, source_target_pairs={{0,4},{4,0},{8,12},{12,8},{16,20},{20,16},{24,28},{28,24},{32,36},... | collective-permute-start | bytes 393224 | tf_op jit(solution)/shard_map/ppermute | solution.py:394
  72.6 6.9 %collective-permute-start.9 = (bf16[128,512]{1,0:T(8,128)(2,1)S(1)}, bf16[128,512]{1,0:T(8,128)(2,1)S(1)}, u32[]{:S(2)}, u32[]{:S(2)}) collective-permute-start(bf16[128,512]{1,0:T(8,128)(2,1)S(1)} %shard_map.90), channel_id=1, source_target_pairs={{0,248},{4,252},{8,192},{12,196},{16,200},{20,204},{24,208},{28,21... | collective-permute-start | bytes 393224 | tf_op jit(solution)/shard_map/ppermute | solution.py:348
  72.7 8.8 %collective-permute-start.8 = (bf16[128,512]{1,0:T(8,128)(2,1)S(1)}, bf16[128,512]{1,0:T(8,128)(2,1)S(1)}, u32[]{:S(2)}, u32[]{:S(2)}) collective-permute-start(bf16[128,512]{1,0:T(8,128)(2,1)S(1)} %shard_map.90), channel_id=1, source_target_pairs={{0,192},{4,196},{8,200},{12,204},{16,208},{20,212},{24,216},{28,22... | collective-permute-start | bytes 393224 | tf_op jit(solution)/shard_map/ppermute | solution.py:348
  81.5 2.3 %collective-permute-start.10 = (bf16[128,512]{1,0:T(8,128)(2,1)S(1)}, bf16[128,512]{1,0:T(8,128)(2,1)S(1)}, u32[]{:S(2)}, u32[]{:S(2)}) collective-permute-start(bf16[128,512]{1,0:T(8,128)(2,1)S(1)} %shard_map.91), channel_id=1, source_target_pairs={{0,4},{4,0},{8,12},{12,8},{16,20},{20,16},{24,28},{28,24},{32,36},... | collective-permute-start | bytes 393224 | tf_op jit(solution)/shard_map/ppermute | solution.py:394
  103.4 4.8 %collective-permute-start.19 = (bf16[16,8,384]{2,1,0:T(8,128)(2,1)S(1)}, bf16[16,8,384]{2,1,0:T(8,128)(2,1)S(1)}, u32[]{:S(2)}, u32[]{:S(2)}) collective-permute-start(bf16[16,8,384]{2,1,0:T(8,128)(2,1)S(1)} %get-tuple-element.34), channel_id=1, source_target_pairs={{0,1},{1,2},{2,3},{3,0},{4,5},{5,6},{6,7},{7,4},{8,9},{9,10},{10,1... | collective-permute-start | bytes 294920 | tf_op jit(solution)/shard_map/ppermute | solution.py:352
  104.6 6.0 %collective-permute-start.20 = (bf16[16,8,384]{2,1,0:T(8,128)(2,1)S(1)}, bf16[16,8,384]{2,1,0:T(8,128)(2,1)S(1)}, u32[]{:S(2)}, u32[]{:S(2)}) collective-permute-start(bf16[16,8,384]{2,1,0:T(8,128)(2,1)S(1)} %get-tuple-element.35), channel_id=1, source_target_pairs={{0,2},{1,3},{2,0},{3,1},{4,6},{5,7},{6,4},{7,5},{8,10},{9,11},{10,... | collective-permute-start | bytes 294920 | tf_op jit(solution)/shard_map/ppermute | solution.py:352
  105.4 6.2 %collective-permute-start.21 = (bf16[16,8,384]{2,1,0:T(8,128)(2,1)S(1)}, bf16[16,8,384]{2,1,0:T(8,128)(2,1)S(1)}, u32[]{:S(2)}, u32[]{:S(2)}) collective-permute-start(bf16[16,8,384]{2,1,0:T(8,128)(2,1)S(1)} %get-tuple-element.36), channel_id=1, source_target_pairs={{0,3},{1,0},{2,1},{3,2},{4,7},{5,4},{6,5},{7,6},{8,11},{9,8},{10,9... | collective-permute-start | bytes 294920 | tf_op jit(solution)/shard_map/ppermute | solution.py:352
  123.7 5.9 %collective-permute-start.24 = (bf16[16,8,384]{2,1,0:T(8,128)(2,1)S(1)}, bf16[16,8,384]{2,1,0:T(8,128)(2,1)S(1)}, u32[]{:S(2)}, u32[]{:S(2)}) collective-permute-start(bf16[16,8,384]{2,1,0:T(8,128)(2,1)S(1)} %all_to_all.11.refs_0_), channel_id=1, source_target_pairs={{0,2},{1,3},{2,0},{3,1},{4,6},{5,7},{6,4},{7,5},{8,10},{9,11},{10,... | collective-permute-start | bytes 294920 | tf_op jit(solution)/shard_map/ppermute | solution.py:352
  125.3 6.8 %collective-permute-start.23 = (bf16[16,8,384]{2,1,0:T(8,128)(2,1)S(1)}, bf16[16,8,384]{2,1,0:T(8,128)(2,1)S(1)}, u32[]{:S(2)}, u32[]{:S(2)}) collective-permute-start(bf16[16,8,384]{2,1,0:T(8,128)(2,1)S(1)} %all_to_all.11.refs_0_), channel_id=1, source_target_pairs={{0,3},{1,0},{2,1},{3,2},{4,7},{5,4},{6,5},{7,6},{8,11},{9,8},{10,9... | collective-permute-start | bytes 294920 | tf_op jit(solution)/shard_map/ppermute | solution.py:352
  126.5 6.6 %collective-permute-start.22 = (bf16[16,8,384]{2,1,0:T(8,128)(2,1)S(1)}, bf16[16,8,384]{2,1,0:T(8,128)(2,1)S(1)}, u32[]{:S(2)}, u32[]{:S(2)}) collective-permute-start(bf16[16,8,384]{2,1,0:T(8,128)(2,1)S(1)} %all_to_all.11.refs_0_), channel_id=1, source_target_pairs={{0,1},{1,2},{2,3},{3,0},{4,5},{5,6},{6,7},{7,4},{8,9},{9,10},{10,1... | collective-permute-start | bytes 294920 | tf_op jit(solution)/shard_map/ppermute | solution.py:352
